TPU v7x, 1024 devices: a whole 4x8x16 slice. The times are simulated.
1024 devices in a mesh: energy: 64 (over x, y, core), space: 16 (over z).
Axes of the slice: x: 4, y: 8, z: 16, core: 2. Of those that a mesh axis runs over, the one named last changes fastest.
Arguments:
- chain_map: float32 [2, 6144, 384], P(None, 'space'), may hold values from -0.21875 to 0.21875
- chain_source: float32 [2, 2048, 6144], P(None, 'energy', 'space'), may hold values from -4 to 4
- local_map: float32 [2, 6144, 768], P(None, 'space'), may hold values from -0.21875 to 0.21875
- local_source: float32 [2, 12288, 2048], P(None, 'space', 'energy'), may hold values from -6 to 6
- interaction: float32 [2, 16384, 2048], P(None, 'space', 'energy'), may hold values from -6 to 6
- element_pairs: int32 [2, 16384], P(None, 'space'), may hold values from 0 to 767, as said below
Outputs:
- self_energy: float32 [2, 16384, 2048], P(None, 'space', 'energy')
Inputs may be any that keep to these rules, and one draw needn't show every extreme that they name: `element_pairs`: both orbitals of a selected element lie in the same block of 384 orbitals or in neighbouring blocks of its partition.
All inputs are finite; a program needn't handle non-finite values.
Results may differ from a plain program's by a relative error of at most 0.00011.
Values sent between devices are 32-bit elements; how exact they have to be, the bound alone decides.
No kernel may reach another device: no remote copies, remote signals or barrier semaphores. Data moves between devices by JAX's collectives and lax.ppermute only.
A program may use at most 64 MiB of HBM per device.

v0:
```python
import math

import jax
import jax.numpy as jnp
from jax import lax
from jax.sharding import PartitionSpec as P

highest = lax.Precision.HIGHEST


def entering(value, axis, join, neutral):
    count, mine = (lax.axis_size(axis), lax.axis_index(axis))
    pieces = jax.tree.map(lambda part: lax.all_gather(part, axis), value)
    running = jax.tree.map(
        lambda part, zero: jnp.full_like(part, 0) + jnp.asarray(zero, part.dtype), value, neutral
    )

    def step(position, running):
        longer = join(running, jax.tree.map(lambda part: part[position], pieces))
        return jax.tree.map(lambda new, old: jnp.where(position < mine, new, old), longer, running)

    return lax.fori_loop(0, count - 1, step, running)


def complex_dot(left_part, right_part):

    def single(first_part, second_part):
        return jnp.dot(
            first_part, second_part, precision=highest, preferred_element_type=jnp.float32
        )

    real_part = single(left_part[0], right_part[0]) - single(left_part[1], right_part[1])
    imag_part = single(left_part[0], right_part[1]) + single(left_part[1], right_part[0])
    return jnp.stack([real_part, imag_part])


def spread_dot(weights, states):
    count = states.shape[1]
    width = weights.shape[1]
    stacked_weights = weights.reshape(2 * width, weights.shape[2])
    upper = jnp.concatenate([states[0].T, states[1].T], axis=1)
    lower = jnp.concatenate([-states[1].T, states[0].T], axis=1)
    stacked_states = jnp.concatenate([upper, lower], axis=0)
    product = lax.dot_general(
        stacked_weights,
        stacked_states,
        (((0,), (0,)), ((), ())),
        precision=highest,
        preferred_element_type=jnp.float32,
    )
    return jnp.stack([product[:, :count], product[:, count:]])


def phase_table(row_count, col_count, period, direction):
    product = (
        lax.broadcasted_iota(jnp.int32, (row_count, col_count), 0)
        * lax.broadcasted_iota(jnp.int32, (row_count, col_count), 1)
        % period
    )
    angles = direction * 2.0 * math.pi / period * product.astype(jnp.float32)
    return (jnp.cos(angles), jnp.sin(angles))


def complex_einsum(pattern, left_pair, right_pair):

    def single(first_part, second_part):
        return jnp.einsum(
            pattern, first_part, second_part, precision=highest, preferred_element_type=jnp.float32
        )

    real_part = single(left_pair[0], right_pair[0]) - single(left_pair[1], right_pair[1])
    imag_part = single(left_pair[0], right_pair[1]) + single(left_pair[1], right_pair[0])
    return (real_part, imag_part)


def complex_times(left_pair, right_pair):
    real_part = left_pair[0] * right_pair[0] - left_pair[1] * right_pair[1]
    imag_part = left_pair[0] * right_pair[1] + left_pair[1] * right_pair[0]
    return (real_part, imag_part)


def split_sizes(length):
    inner_size = 128
    return (length // inner_size, inner_size)


def forward_transform(real_part, imag_part):
    length = real_part.shape[-1]
    outer_size, inner_size = split_sizes(length)
    sectioned = (
        real_part.reshape(-1, outer_size, inner_size),
        imag_part.reshape(-1, outer_size, inner_size),
    )
    sectioned = complex_einsum(
        "mab,ak->mkb", sectioned, phase_table(outer_size, outer_size, outer_size, -1.0)
    )
    sectioned = complex_times(sectioned, phase_table(outer_size, inner_size, length, -1.0))
    return complex_einsum(
        "mkb,bq->mkq", sectioned, phase_table(inner_size, inner_size, inner_size, -1.0)
    )


def inverse_transform(spectrum, length):
    outer_size, inner_size = split_sizes(length)
    sectioned = complex_einsum(
        "mkq,qb->mkb", spectrum, phase_table(inner_size, inner_size, inner_size, 1.0)
    )
    sectioned = complex_times(sectioned, phase_table(outer_size, inner_size, length, 1.0))
    sectioned = complex_einsum(
        "mkb,ka->mab", sectioned, phase_table(outer_size, outer_size, outer_size, 1.0)
    )
    return (sectioned[0].reshape(-1, length) / length, sectioned[1].reshape(-1, length) / length)


def correlate(pieces):
    lesser, screened = pieces
    layout = lesser.shape
    length = layout[-1]
    lesser_spec = forward_transform(lesser[0].reshape(-1, length), lesser[1].reshape(-1, length))
    screened_spec = forward_transform(
        screened[0].reshape(-1, length), screened[1].reshape(-1, length)
    )
    response_re, response_im = inverse_transform(complex_times(lesser_spec, screened_spec), length)
    factor = length ** (-0.5)
    response = jnp.stack([response_re * factor, response_im * factor]).reshape(layout)
    return lax.all_to_all(response, "energy", split_axis=3, concat_axis=1, tiled=True)


def body(chain_map, chain_source, local_map, local_source, interaction, element_pairs):

    def compose(earlier_map, later_map):
        return (
            complex_dot(earlier_map[0], later_map[0]),
            complex_dot(earlier_map[1], later_map[0]) + later_map[1],
        )

    unit_matrix = jnp.eye(chain_map.shape[1], dtype=jnp.float32)
    identity = (jnp.stack([unit_matrix, jnp.zeros_like(unit_matrix)]), jnp.zeros_like(chain_source))
    prefix = entering((chain_map, chain_source), "space", compose, identity)
    incoming = prefix[1]
    wavefunction = spread_dot(local_map, incoming) + local_source
    left_rows = jnp.take(wavefunction, element_pairs[0], axis=1)
    right_rows = jnp.take(wavefunction, element_pairs[1], axis=1)
    lesser_re = left_rows[0] * right_rows[0] + left_rows[1] * right_rows[1]
    lesser_im = left_rows[1] * right_rows[0] - left_rows[0] * right_rows[1]
    groups = lax.axis_size("energy")
    selected, energies = lesser_re.shape
    lesser = jnp.stack([lesser_re, lesser_im]).reshape(2, groups, selected // groups, energies)
    screened = interaction.reshape(2, groups, selected // groups, energies)
    self_energy = correlate(
        (
            lax.all_to_all(lesser, "energy", split_axis=1, concat_axis=3, tiled=True),
            lax.all_to_all(screened, "energy", split_axis=1, concat_axis=3, tiled=True),
        )
    )
    return self_energy.reshape(2, selected, energies)


def solution(mesh):
    in_specs = (
        P(None, "space", None),
        P(None, "energy", "space"),
        P(None, "space", None),
        P(None, "space", "energy"),
        P(None, "space", "energy"),
        P(None, "space"),
    )
    out_specs = P(None, "space", "energy")
    return jax.shard_map(body, mesh=mesh, in_specs=in_specs, out_specs=out_specs, check_vma=False)
```

profile of v0, /device:TPU:1, one launch (start us, length us, event | category | flops | bytes accessed | tf_op | source)
XLA Modules:
  0.0 520.3 jit_solution(6018363623330832303)
XLA Ops:
  8.0 2.3 copy.39
  12.8 18.2 %all-to-all-start.1 = ((f32[64,1,1024]{2,1,0:T(1,128)}), f32[64,1,1024]{2,1,0:T(1,128)S(1)}, u32[]{:S(2)}, u32[]{:S(2)}) async-start(f32[64,1,1024]{2,1,0:T(1,128)} %reshape.134), calls=%async_computation.1 | async-start | bytes 524288 | tf_op jit(solution)/shard_map/all_to_all | solution.py:153
  34.1 8.9 %all-to-all-done.1 = f32[64,1,1024]{2,1,0:T(1,128)S(1)} async-done(((f32[64,1,1024]{2,1,0:T(1,128)}), f32[64,1,1024]{2,1,0:T(1,128)S(1)}, u32[]{:S(2)}, u32[]{:S(2)}) %all-to-all-start.1) | async-done | bytes 262176 | tf_op jit(solution)/shard_map/all_to_all | solution.py:153
  43.6 2.0 reduce
  52.7 31.3 %all-gather.7.cloned.1.call-done = f32[32,32,384]{2,1,0:T(8,128)} async-done(((f32[2,32,384]{2,1,0:T(8,128)}), f32[32,32,384]{2,1,0:T(8,128)}) %all-gather.7.cloned.1.call-update) | async-done | bytes 1572880 | tf_op jit(solution)/shard_map/all_gather | solution.py:13
  83.9 224.5 %all-gather.5.cloned.1.call-done = f32[32,384,384]{2,1,0:T(8,128)} async-done(((f32[2,384,384]{2,1,0:T(8,128)}), f32[32,384,384]{2,1,0:T(8,128)}) %all-gather.5.cloned.1.call-update) | async-done | bytes 18874384 | tf_op jit(solution)/shard_map/all_gather | solution.py:13
  308.5 106.0 %while.14 = (s32[]{:T(128)}, f32[2,32,384]{2,1,0:T(8,128)S(1)}, s32[]{:T(128)}, f32[16,2,384,384]{3,2,1,0:T(8,128)}, f32[16,2,32,384]{3,2,1,0:T(8,128)}, /*index=5*/s32[]{:T(128)}, s32[]{:T(128)}, s32[]{}) while((s32[]{:T(128)}, f32[2,32,384]{2,1,0:T(8,128)S(1)}, s32[]{:T(128)}, f32[16,2,384,384]{3,2,1,0:T(8,128)}, ...), condition=%wide.region_1.2_spmd.clone, body=%wide.region_0.1_spmd.clone.sunk | while | flops 226639872 | bytes 3442818 | solution.py:22
  310.0 1.5 fusion.251
  311.5 1.5 fusion.248
  313.0 1.5 fusion.249
  317.1 1.5 fusion.251
  318.6 1.5 fusion.248
  320.1 1.5 fusion.249
  324.1 1.5 fusion.251
  325.7 1.5 fusion.248
  327.2 1.5 fusion.249
  331.2 1.5 fusion.251
  332.7 1.5 fusion.248
  334.2 1.5 fusion.249
  338.3 1.5 fusion.251
  339.8 1.5 fusion.248
  341.3 1.5 fusion.249
  345.3 1.5 fusion.251
  346.9 1.5 fusion.248
  348.4 1.5 fusion.249
  352.4 1.5 fusion.251
  353.9 1.5 fusion.248
  355.4 1.5 fusion.249
  359.5 1.5 fusion.251
  361.0 1.5 fusion.248
  362.5 1.5 fusion.249
  366.5 1.5 fusion.251
  368.1 1.5 fusion.248
  369.6 1.5 fusion.249
  373.6 1.5 fusion.251
  375.1 1.5 fusion.248
  376.6 1.5 fusion.249
  380.7 1.5 fusion.251
  382.2 1.5 fusion.248
  383.7 1.5 fusion.249
  387.7 1.5 fusion.251
  389.2 1.5 fusion.248
  390.8 1.5 fusion.249
  394.8 1.5 fusion.251
  396.3 1.5 fusion.248
  401.9 1.5 fusion.251
  403.4 1.5 fusion.248
  408.9 1.5 fusion.251
  410.4 1.5 fusion.248
  414.5 1.5 convolution_bitcast_fusion
  416.6 7.5 %gather_fusion = f32[1024,2,32]{2,1,0:T(2,128)} fusion(f32[2,768,32]{2,0,1:T(2,128)S(1)} %copy.34, s32[1024]{0:T(1024)S(1)} %copy-done.7), kind=kCustom, calls=%fused_computation.clone | custom fusion | bytes 528384 | tf_op jit(solution)/shard_map/jit(_take)/gather | solution.py:142
  424.1 7.5 %gather_fusion.1 = f32[1024,2,32]{2,1,0:T(2,128)} fusion(f32[2,768,32]{2,0,1:T(2,128)S(1)} %copy.34, s32[1024]{0:T(1024)S(1)} %copy-done.8), kind=kCustom, calls=%fused_computation.1.clone | custom fusion | bytes 528384 | tf_op jit(solution)/shard_map/jit(_take)/gather | solution.py:143
  431.7 6.1 %select_bitcast_fusion = (f32[2,1024,32]{2,0,1:T(2,128)S(1)}, f32[2,1024,32]{2,0,1:T(2,128)S(1)}) fusion(f32[1024,2,32]{2,1,0:T(2,128)} %gather_fusion.1, pred[1024]{0:T(1024)(128)(4,1)S(1)} %copy-done.10, f32[1024,2,32]{2,1,0:T(2,128)} %gather_fusion, pred[1024]{0:T(1024)(128)(4,1)S(1)} %copy-done.11), kind=kLoop, calls=%fused_computation.37 | loop fusion | flops 131072 | bytes 1050624 | tf_op jit(solution)/shard_map/jit(_take)/select_n | solution.py:143
  440.5 10.5 %all-to-all-start = ((f32[64,1,1024]{2,1,0:T(1,128)}), f32[64,1,1024]{2,1,0:T(1,128)S(1)}, u32[]{:S(2)}, u32[]{:S(2)}) async-start(f32[64,1,1024]{2,1,0:T(1,128)} %reshape.132), calls=%async_computation | async-start | bytes 524288 | tf_op jit(solution)/shard_map/all_to_all | solution.py:152
  452.4 2.1 convolution_add_fusion.3
  454.6 2.1 convolution_subtract_fusion.3
  456.6 6.3 %all-to-all-done = f32[64,1,1024]{2,1,0:T(1,128)S(1)} async-done(((f32[64,1,1024]{2,1,0:T(1,128)}), f32[64,1,1024]{2,1,0:T(1,128)S(1)}, u32[]{:S(2)}, u32[]{:S(2)}) %all-to-all-start) | async-done | bytes 262176 | tf_op jit(solution)/shard_map/all_to_all | solution.py:152
  463.0 2.0 reduce.1
  477.2 2.3 copy.43
  479.4 2.6 bitcast_bitcast_fusion
  482.1 4.4 reshape.136
  486.5 17.8 %all_to_all.45 = f32[64,1,1024]{2,1,0:T(1,128)S(1)} all-to-all(f32[64,1,1024]{2,1,0:T(1,128)S(1)} %reshape.136), channel_id=1, replica_groups=mesh['energy'=64,'space'=16] {'energy'}, dimensions={0} | all-to-all | bytes 524288 | tf_op jit(solution)/shard_map/all_to_all | solution.py:126
  505.6 4.1 reshape.137
  509.7 2.7 copy.48
  (136 shorter events, 74.8 us)
Async XLA Ops:
  6.5 408.0 %copy-start = (f32[2,384,768]{2,1,0:T(8,128)S(1)}, f32[2,384,768]{2,1,0:T(8,128)}, u32[]{:S(2)}) copy-start(f32[2,384,768]{2,1,0:T(8,128)} %param.12) | copy-start | bytes 7077892
  6.5 77.4 %all-gather.7.cloned.1.call-start = ((), (), s32[]{:S(2)}) async-start(), calls=%async_computation.4 | async-start | bytes 1671168 | tf_op jit(solution)/shard_map/all_gather | solution.py:13
  7.3 301.2 %all-gather.5.cloned.1.call-start = ((), (), s32[]{:S(2)}) async-start(), calls=%async_computation.3 | async-start | bytes 20054016 | tf_op jit(solution)/shard_map/all_gather | solution.py:13
  8.0 23.1 %copy-start.9 = (s32[2,1024]{1,0:T(2,128)S(1)}, s32[2,1024]{1,0:T(2,128)}, u32[]{:S(2)}) copy-start(s32[2,1024]{1,0:T(2,128)} %param.15) | copy-start | bytes 24580
  12.8 30.2 %all-to-all-start.1 = ((f32[64,1,1024]{2,1,0:T(1,128)}), f32[64,1,1024]{2,1,0:T(1,128)S(1)}, u32[]{:S(2)}, u32[]{:S(2)}) async-start(f32[64,1,1024]{2,1,0:T(1,128)} %reshape.134), calls=%async_computation.1 | async-start | bytes 524288 | tf_op jit(solution)/shard_map/all_to_all | solution.py:153
  51.5 257.0 %copy-start.1 = (f32[16,16,128]{2,0,1:T(8,128)}, f32[16,16,128]{2,0,1:T(8,128)S(1)}, u32[]{:S(2)}) copy-start(f32[16,16,128]{2,0,1:T(8,128)S(1)} %convolution_add_fusion.5) | copy-start | bytes 393220
  414.4 1.6 copy-start.6
  414.5 2.1 copy-start.7
  416.0 8.1 %copy-start.8 = (s32[1024]{0:T(1024)S(1)}, s32[1024]{0:T(1024)}, u32[]{:S(2)}) copy-start(s32[1024]{0:T(1024)} %fusion.128) | copy-start | bytes 12292
  416.1 15.6 %copy-start.10 = (pred[1024]{0:T(1024)(128)(4,1)S(1)}, pred[1024]{0:T(1024)(128)(4,1)}, u32[]{:S(2)}) copy-start(pred[1024]{0:T(1024)(128)(4,1)} %compare_and_fusion) | copy-start | bytes 3076
  416.1 15.6 %copy-start.11 = (pred[1024]{0:T(1024)(128)(4,1)S(1)}, pred[1024]{0:T(1024)(128)(4,1)}, u32[]{:S(2)}) copy-start(pred[1024]{0:T(1024)(128)(4,1)} %compare_and_fusion.1) | copy-start | bytes 3076
  440.5 22.5 %all-to-all-start = ((f32[64,1,1024]{2,1,0:T(1,128)}), f32[64,1,1024]{2,1,0:T(1,128)S(1)}, u32[]{:S(2)}, u32[]{:S(2)}) async-start(f32[64,1,1024]{2,1,0:T(1,128)} %reshape.132), calls=%async_computation | async-start | bytes 524288 | tf_op jit(solution)/shard_map/all_to_all | solution.py:152
  468.7 4.4 copy-start.2
  468.9 4.2 copy-start.3
  469.1 6.7 %copy-start.4 = (f32[16,128]{1,0:T(8,128)S(1)}, f32[16,128]{1,0:T(8,128)}, u32[]{:S(2)}) copy-start(f32[16,128]{1,0:T(8,128)} %get-tuple-element.147) | copy-start | bytes 24580
  469.1 6.7 %copy-start.5 = (f32[16,128]{1,0:T(8,128)S(1)}, f32[16,128]{1,0:T(8,128)}, u32[]{:S(2)}) copy-start(f32[16,128]{1,0:T(8,128)} %get-tuple-element.148) | copy-start | bytes 24580
Sparse Core Ops, SparseCore 0:
  10.0 73.8 all-gather.6
  86.6 221.8 all-gather.4
where the time goes:
time: 524 us; the launch traced here: 520 us
  waiting for transfers between devices  272 us (52%)
  matrix products  112 us (21%)
  local copies, waits for them, and re-layouts  44.2 us (8%)
  other arithmetic  30.1 us (6%)
  starting transfers between devices  28.8 us (5%)
  blocking collectives  17.8 us (3%)
  between operations  13.9 us (3%)
    all_gather x2, waiting for transfers between devices, entering(): pieces = jax.tree.map(lambda part: lax.all_gather(part, axis), value)  256 us
    dot_general x60, matrix products, single(): jnp.dot(first_part, second_part, precision=highest, preferred_element_typ...  90.9 us
    dot_general x24, matrix products, single(): jnp.einsum(pattern, first_part, second_part, precision=highest, preferred...  19.6 us
    unnamed x32, local copies, waits for them, and re-layouts  18.4 us
    all_to_all x1, starting transfers between devices, body(): lax.all_to_all(screened, 'energy', split_axis=1, concat_axis=3, tiled=True)  18.2 us
    all_to_all x1, blocking collectives, correlate(): lax.all_to_all(response, 'energy', split_axis=3, concat_axis=1, tiled=True)  17.8 us
    select_n x15, other arithmetic, step(): jnp.where(position < mine, new, old)  13.9 us
    all_to_all x1, starting transfers between devices, body(): lax.all_to_all(lesser, 'energy', split_axis=1, concat_axis=3, tiled=True)  10.5 us
  transfers between devices with their start and end apart: 4, of which 4 were waited for; matrix products, arithmetic and copies ran while one was open for 4% of the time, Pallas kernels for 0%

commit v1 on v0

v1 whole, which is shorter than its diff:
```python
import jax
import jax.numpy as jnp
import numpy as np
from jax import lax
from jax.experimental import pallas as pl
from jax.experimental.pallas import tpu as pltpu
from jax.sharding import PartitionSpec as P

f32 = jnp.float32
bf16 = jnp.bfloat16


def call(kernel, out_shape, name, megabytes, scratch=()):
    return pl.pallas_call(
        kernel,
        out_shape=out_shape,
        scratch_shapes=list(scratch),
        name=name,
        compiler_params=pltpu.CompilerParams(vmem_limit_bytes=megabytes << 20),
    )


def halves(value):
    high = value.astype(bf16)
    return high, (value - high.astype(f32)).astype(bf16)


def dot(left, right):
    return jnp.dot(left, right, preferred_element_type=f32)


def complex_rows_dot(rows, high_ref, low_ref):
    count = rows.shape[0]
    high, low = halves(rows)
    both = dot(jnp.concatenate([high, low], axis=0), high_ref[...])
    product = both[:count] + both[count:] + dot(high, low_ref[...])
    half, width = count // 2, product.shape[1] // 2
    real = product[:half, :width] - product[half:, width:]
    imag = product[:half, width:] + product[half:, :width]
    return real, imag


def split_kernel(map_ref, high_ref, low_ref):
    width = map_ref.shape[2]
    for part in range(2):
        high, low = halves(map_ref[part])
        high_ref[:, part * width : (part + 1) * width] = high
        low_ref[:, part * width : (part + 1) * width] = low


def split_map(value):
    shape = jax.ShapeDtypeStruct((value.shape[1], 2 * value.shape[2]), bf16)
    return call(split_kernel, [shape, shape], "split_map", 8)(value)


def step_kernel(arrived_ref, state_ref, entering_ref, high_ref, low_ref, state_out, entering_out):
    arrived = arrived_ref[...]
    half = arrived.shape[0] // 2
    entering_out[...] = entering_ref[...] + arrived
    real, imag = complex_rows_dot(arrived, high_ref, low_ref)
    state_out[:half] = state_ref[:half] + real
    state_out[half:] = state_ref[half:] + imag


def chain_step(arrived, state, entering, high, low):
    shape = jax.ShapeDtypeStruct(state.shape, f32)
    return call(step_kernel, [shape, shape], "chain_step", 6)(arrived, state, entering, high, low)


def swap_blocks(parts):
    block = lax.broadcasted_iota(jnp.int32, parts[0].shape, 1) // 16
    for step in (1, 2, 4):
        clear = (block & step) == 0
        swapped = list(parts)
        for place in range(8):
            if place & step == 0:
                lower, upper = parts[place], parts[place + step]
                swapped[place] = jnp.where(clear, lower, pltpu.roll(upper, 16 * step, 1))
                swapped[place + step] = jnp.where(clear, pltpu.roll(lower, 128 - 16 * step, 1), upper)
        parts = swapped
    return parts


def pack(stage_ref, packed_ref):
    for group in range(8):
        parts = [stage_ref[b // 4, group, pl.ds(b % 4, 8, stride=4), :] for b in range(8)]
        for place, tile in enumerate(swap_blocks(parts)):
            packed_ref[8 * group + place] = tile


def pack_kernel(values_ref, packed_ref, stage_ref):
    for part in range(2):
        for group in range(8):
            stage_ref[part, group] = values_ref[part, :, group * 128 : (group + 1) * 128]
    pack(stage_ref, packed_ref)


def unpack_kernel(packed_ref, values_ref, stage_ref):
    for group in range(8):
        parts = [packed_ref[8 * group + place] for place in range(8)]
        for b, tile in enumerate(swap_blocks(parts)):
            stage_ref[b // 4, group, pl.ds(b % 4, 8, stride=4), :] = tile
    for part in range(2):
        for group in range(8):
            values_ref[part, :, group * 128 : (group + 1) * 128] = stage_ref[part, group]


def pack_array(values):
    shape = jax.ShapeDtypeStruct((64, 8, 128), f32)
    return call(pack_kernel, shape, "pack_screened", 4, [pltpu.VMEM((2, 8, 32, 128), f32)])(values)


def unpack_array(packed):
    shape = jax.ShapeDtypeStruct((2, 32, 1024), f32)
    return call(unpack_kernel, shape, "unpack_result", 4, [pltpu.VMEM((2, 8, 32, 128), f32)])(packed)


def choose_kernel(pairs_ref, chosen_ref):
    orbitals, count = chosen_ref.shape[0], pairs_ref.shape[1]
    for side in range(2):
        for group in range(count // 128):
            wanted = pairs_ref[side : side + 1, group * 128 : (group + 1) * 128]
            rows = lax.broadcasted_iota(jnp.int32, (orbitals, 128), 0)
            column = side * count + group * 128
            chosen_ref[:, column : column + 128] = jnp.where(rows == wanted, 1.0, 0.0).astype(bf16)


def choose(pairs, orbitals):
    shape = jax.ShapeDtypeStruct((orbitals, 2 * pairs.shape[1]), bf16)
    return call(choose_kernel, shape, "choose", 8)(pairs)


def lesser_kernel(
    arrived_ref, entering_ref, high_ref, low_ref, source_ref, chosen_ref, packed_ref, stage_ref
):
    state = entering_ref[...] + arrived_ref[...]
    real, imag = complex_rows_dot(state, high_ref, low_ref)
    wave = jnp.concatenate([real + source_ref[0], imag + source_ref[1]], axis=0)
    rows, half = wave.shape[0], wave.shape[0] // 2
    high, low = halves(wave)
    both = dot(jnp.concatenate([high, low], axis=0), chosen_ref[...])
    taken = both[:rows] + both[rows:]
    count = taken.shape[1] // 2
    left_re, left_im = taken[:half, :count], taken[half:, :count]
    right_re, right_im = taken[:half, count:], taken[half:, count:]
    lesser_re = left_re * right_re + left_im * right_im
    lesser_im = left_im * right_re - left_re * right_im
    for group in range(8):
        stage_ref[0, group] = lesser_re[:, group * 128 : (group + 1) * 128]
        stage_ref[1, group] = lesser_im[:, group * 128 : (group + 1) * 128]
    pack(stage_ref, packed_ref)


def packed_lesser(arrived, entering, high, low, source, chosen):
    shape = jax.ShapeDtypeStruct((64, 8, 128), f32)
    scratch = [pltpu.VMEM((2, 8, 32, 128), f32)]
    return call(lesser_kernel, shape, "packed_lesser", 14, scratch)(
        arrived, entering, high, low, source, chosen
    )


def small_tables():
    coarse, fine = 32 * np.arange(16)[:, None], np.arange(32)[:, None]
    column, lane = np.arange(512)[None, :], np.arange(128)
    imaginary, phase, element = lane // 64, lane // 16 % 4, lane % 16

    def both(rows, columns, period):
        angle = 2.0 * np.pi / period * (rows * columns % period)
        return np.stack([np.cos(angle), np.sin(angle)]).astype(np.float32)

    turns = phase[:, None] * phase[None, :] % 4
    cosine, sine = np.array([1, 0, -1, 0])[turns], np.array([0, 1, 0, -1])[turns]
    sign = imaginary[:, None] - imaginary[None, :]
    same = element[:, None] == element[None, :]
    forward = np.where(sign == 0, cosine, sign * sine) * same
    backward = np.where(sign == 0, cosine, -sign * sine) * same
    lanes = np.stack([forward, backward]).astype(jnp.bfloat16)
    return (
        both(coarse, column, 512),
        both(fine, column, 512),
        both(coarse, phase[None, :], 2048),
        both(fine, phase[None, :], 2048),
        lanes,
    )


def tables_kernel(coarse_ref, fine_ref, outer_ref, inner_ref, high_ref, low_ref, twiddle_ref):
    lane = lax.broadcasted_iota(jnp.int32, (32, 128), 1)
    for place in range(16):
        rows = slice(32 * place, 32 * place + 32)
        cosine, sine = coarse_ref[0, place : place + 1], coarse_ref[1, place : place + 1]
        high, low = halves(cosine * fine_ref[0] - sine * fine_ref[1])
        high_ref[rows, :512], low_ref[rows, :512] = high, low
        high, low = halves(sine * fine_ref[0] + cosine * fine_ref[1])
        high_ref[rows, 512:], low_ref[rows, 512:] = high, low
        cosine, sine = outer_ref[0, place : place + 1], outer_ref[1, place : place + 1]
        twiddle_ref[0, rows] = cosine * inner_ref[0] - sine * inner_ref[1]
        turn = sine * inner_ref[0] + cosine * inner_ref[1]
        twiddle_ref[1, rows] = jnp.where(lane < 64, turn, -turn)


def tables():
    *small, lanes = small_tables()
    waves = jax.ShapeDtypeStruct((512, 1024), bf16)
    shapes = [waves, waves, jax.ShapeDtypeStruct((2, 512, 128), f32)]
    return (*call(tables_kernel, shapes, "tables", 8)(*small), lanes)


def turned(value):
    lane = lax.broadcasted_iota(jnp.int32, value.shape, 1)
    rolled = pltpu.roll(value, 64, 1)
    return jnp.where(lane < 64, rolled, -rolled)


def rows_transform(value, other, high_ref, low_ref):
    high, low = halves(jnp.concatenate([value, other], axis=0))
    both = dot(high_ref[...], jnp.concatenate([high, low], axis=1))
    return both[:, :128] + both[:, 128:] + dot(low_ref[...], high)


def lanes_transform(value, table):
    high, low = halves(value)
    return dot(high, table) + dot(low, table)


def spectrum_of(packed_ref, high_ref, low_ref, twiddle_ref, lanes_ref):
    value = packed_ref[...].reshape(512, 128)
    value = rows_transform(value, turned(value), high_ref, low_ref)
    value = value * twiddle_ref[0] + pltpu.roll(value, 64, 1) * twiddle_ref[1]
    return lanes_transform(value, lanes_ref[0])


def screened_kernel(packed_ref, high_ref, low_ref, twiddle_ref, lanes_ref, out_ref):
    value = spectrum_of(packed_ref, high_ref, low_ref, twiddle_ref, lanes_ref) * (2048.0**-1.5)
    rolled = pltpu.roll(value, 64, 1)
    first = lax.broadcasted_iota(jnp.int32, value.shape, 1) < 64
    out_ref[0] = jnp.where(first, value, rolled)
    out_ref[1] = jnp.where(first, -rolled, value)


def convolve_kernel(packed_ref, screened_ref, high_ref, low_ref, twiddle_ref, lanes_ref, out_ref):
    value = spectrum_of(packed_ref, high_ref, low_ref, twiddle_ref, lanes_ref)
    value = value * screened_ref[0] + pltpu.roll(value, 64, 1) * screened_ref[1]
    value = lanes_transform(value, lanes_ref[1])
    value = value * twiddle_ref[0] - pltpu.roll(value, 64, 1) * twiddle_ref[1]
    value = rows_transform(value, -turned(value), high_ref, low_ref)
    out_ref[...] = value.reshape(64, 8, 128)


def screened_spectrum(packed, constants):
    shape = jax.ShapeDtypeStruct((2, 512, 128), f32)
    return call(screened_kernel, shape, "screened_spectrum", 8)(packed, *constants)


def convolve(packed, screened, constants):
    shape = jax.ShapeDtypeStruct((64, 8, 128), f32)
    return call(convolve_kernel, shape, "convolve", 8)(packed, screened, *constants)


def exchange(packed):
    return lax.all_to_all(packed, "energy", split_axis=0, concat_axis=0, tiled=True)


def body(chain_map, chain_source, local_map, local_source, interaction, element_pairs):
    constants = tables()
    partitions = lax.axis_size("space")
    rows = 2 * chain_source.shape[1]
    state = chain_source.reshape(rows, chain_source.shape[2])
    entering = jnp.zeros_like(state)
    map_high, map_low = split_map(chain_map)
    for place in range(1, partitions):
        arrived = lax.ppermute(state, "space", [(place - 1, place)])
        if place < partitions - 1:
            state, entering = chain_step(arrived, state, entering, map_high, map_low)
    screened = exchange(pack_array(jnp.swapaxes(interaction, 1, 2)))
    screened = screened_spectrum(screened, constants)
    local_high, local_low = split_map(local_map)
    chosen = choose(element_pairs, local_map.shape[2])
    source = jnp.swapaxes(local_source, 1, 2)
    packed = packed_lesser(arrived, entering, local_high, local_low, source, chosen)
    result = convolve(exchange(packed), screened, constants)
    return jnp.swapaxes(unpack_array(exchange(result)), 1, 2)


def solution(mesh):
    in_specs = (
        P(None, "space", None),
        P(None, "energy", "space"),
        P(None, "space", None),
        P(None, "space", "energy"),
        P(None, "space", "energy"),
        P(None, "space"),
    )
    out_specs = P(None, "space", "energy")
    return jax.shard_map(body, mesh=mesh, in_specs=in_specs, out_specs=out_specs, check_vma=False)
```

time: 524 us -> 119 us (0.23)
  the two profiles are of different devices: /device:TPU:1 before, /device:TPU:961 now
where the time goes in v1:
time: 119 us; the launch traced here: 118 us
  starting transfers between devices  48.3 us (41%)
  waiting for transfers between devices  34.2 us (29%)
  blocking collectives  17.9 us (15%)
  Pallas kernels  13.9 us (12%)
  local copies, waits for them, and re-layouts  3.61 us (3%)
    all_to_all x2, starting transfers between devices, exchange(): lax.all_to_all(packed, 'energy', split_axis=0, concat_axis=0, tiled=True)  37.6 us
    ppermute x15, waiting for transfers between devices, body(): arrived = lax.ppermute(state, 'space', [(place - 1, place)])  24.9 us
    all_to_all x1, blocking collectives, exchange(): lax.all_to_all(packed, 'energy', split_axis=0, concat_axis=0, tiled=True)  17.9 us
    ppermute x15, starting transfers between devices, body(): arrived = lax.ppermute(state, 'space', [(place - 1, place)])  10.7 us
    all_to_all x2, waiting for transfers between devices, exchange(): lax.all_to_all(packed, 'energy', split_axis=0, concat_axis=0, tiled=True)  9.34 us
    pallas_call x14, Pallas kernels, chain_step(): call(step_kernel, [shape, shape], 'chain_step', 6)  4.46 us
    unnamed x26, local copies, waits for them, and re-layouts  3.6 us
  transfers between devices with their start and end apart: 17, of which 2 were waited for; matrix products, arithmetic and copies ran while one was open for 0% of the time, Pallas kernels for 7%

profile of v1, /device:TPU:961, one launch (start us, length us, event | category | flops | bytes accessed | tf_op | source)
XLA Modules:
  0.0 118.5 jit_solution(17872135277561616554)
XLA Ops:
  0.0 0.7 collective-permute-start
  0.7 1.3 %copy-done.1 = f32[2,384,384]{2,1,0:T(8,128)S(1)} copy-done((f32[2,384,384]{2,1,0:T(8,128)S(1)}, f32[2,384,384]{2,1,0:T(8,128)}, u32[]{:S(2)}) %copy-start.1) | copy-done | bytes 1179672
  1.9 0.2 split_map.2
  2.2 0.0 collective-permute-done.arrived_ref
  2.2 0.6 copy-done.8
  2.8 0.3 chain_step.14
  3.2 0.7 collective-permute-start.1
  3.8 0.0 collective-permute-done.1.arrived_ref
  3.8 0.3 chain_step.15
  4.2 0.7 collective-permute-start.2
  4.8 0.0 collective-permute-done.2.arrived_ref
  4.9 0.3 chain_step.16
  5.2 0.7 collective-permute-start.3
  5.9 0.0 collective-permute-done.3.arrived_ref
  5.9 0.3 chain_step.17
  6.2 0.7 collective-permute-start.4
  6.9 0.0 collective-permute-done.4.arrived_ref
  6.9 0.3 chain_step.18
  7.2 0.7 collective-permute-start.5
  7.9 0.0 collective-permute-done.5.arrived_ref
  7.9 0.3 chain_step.19
  8.2 0.7 collective-permute-start.6
  8.9 0.0 collective-permute-done.6.arrived_ref
  8.9 0.3 chain_step.20
  9.2 0.7 collective-permute-start.7
  9.9 0.0 copy-start.5
  9.9 0.3 chain_step.21
  10.3 0.7 collective-permute-start.8
  10.9 0.0 collective-permute-done.8.arrived_ref
  10.9 0.3 chain_step.22
  11.3 0.7 collective-permute-start.9
  11.9 1.1 pack_screened.1
  13.0 10.8 %all-to-all-start.1 = ((f32[64,8,128]{2,1,0:T(8,128)}), f32[64,8,128]{2,1,0:T(8,128)S(1)}, u32[]{:S(2)}, u32[]{:S(2)}) async-start(f32[64,8,128]{2,1,0:T(8,128)} %pack_screened.1), calls=%async_computation.1 | async-start | bytes 524288 | tf_op jit(solution)/shard_map/all_to_all | solution.py:261
  23.8 0.3 chain_step.23
  24.2 0.7 collective-permute-start.10
  24.9 0.3 chain_step.24
  25.2 0.7 collective-permute-start.11
  25.9 0.0 collective-permute-done.11.arrived_ref
  25.9 0.3 chain_step.25
  26.2 0.7 collective-permute-start.12
  26.9 0.0 collective-permute-done.12.arrived_ref
  26.9 0.0 copy-start
  26.9 0.3 chain_step.26
  27.2 0.8 collective-permute-start.13
  28.0 0.0 collective-permute-done.13.arrived_ref
  28.0 0.3 chain_step.27
  28.4 0.0 copy-start.12
  28.4 1.3 %collective-permute-start.14 = (f32[64,384]{1,0:T(8,128)S(1)}, f32[64,384]{1,0:T(8,128)S(1)}, u32[]{:S(2)}, u32[]{:S(2)}) collective-permute-start(f32[64,384]{1,0:T(8,128)S(1)} %get-tuple-element.68), channel_id=1, source_target_pairs={{14,15},{30,31},{46,47},{62,63},{78,79},{94,95},{110,111},{126,127... | collective-permute-start | bytes 294920 | tf_op jit(solution)/shard_map/ppermute | solution.py:272
  29.7 0.3 split_map.3
  30.0 0.0 copy-start.6
  30.0 1.0 choose.1.chosen_ref
  31.0 24.9 %collective-permute-done.14.arrived_ref = f32[64,384]{1,0:T(8,128)S(1)} collective-permute-done((f32[64,384]{1,0:T(8,128)S(1)}, f32[64,384]{1,0:T(8,128)S(1)}, u32[]{:S(2)}, u32[]{:S(2)}) %collective-permute-start.14) | collective-permute-done | bytes 98336 | tf_op jit(solution)/shard_map/ppermute | solution.py:272
  55.9 0.0 copy-start.11
  55.9 0.0 copy-start.4
  55.9 2.1 %packed_lesser.1 = f32[64,8,128]{2,1,0:T(8,128)} custom-call(f32[64,384]{1,0:T(8,128)S(1)} %collective-permute-done.14.arrived_ref, f32[64,384]{1,0:T(8,128)S(1)} %get-tuple-element.69.entering_ref, bf16[384,1536]{1,0:T(8,128)(2,1)S(1)} %get-tuple-element.70.high_ref, bf16[384,1536]{1,0:T(8,128)(2,1)S(1)} %get-tuple-element.71.low_ref, ...), custom_call_target="tpu_custom_call" | custom-call | tf_op jit(solution)/shard_map/packed_lesser/pallas_call | solution.py:157
  58.1 0.7 copy-done.2
  58.8 26.8 %all-to-all-start = ((f32[64,8,128]{2,1,0:T(8,128)}), f32[64,8,128]{2,1,0:T(8,128)S(1)}, u32[]{:S(2)}, u32[]{:S(2)}) async-start(f32[64,8,128]{2,1,0:T(8,128)} %packed_lesser.1), calls=%async_computation | async-start | bytes 524288 | tf_op jit(solution)/shard_map/all_to_all | solution.py:261
  85.6 0.5 tables.1
  86.2 0.9 copy-done.3
  87.1 1.1 screened_spectrum.1.screened_ref
  88.2 9.3 %all-to-all-done.packed_ref = f32[64,8,128]{2,1,0:T(8,128)S(1)} async-done(((f32[64,8,128]{2,1,0:T(8,128)}), f32[64,8,128]{2,1,0:T(8,128)S(1)}, u32[]{:S(2)}, u32[]{:S(2)}) %all-to-all-start) | async-done | bytes 262176 | tf_op jit(solution)/shard_map/all_to_all | solution.py:261
  97.6 2.0 %convolve.1 = f32[64,8,128]{2,1,0:T(8,128)S(1)} custom-call(f32[64,8,128]{2,1,0:T(8,128)S(1)} %all-to-all-done.packed_ref, f32[2,512,128]{2,1,0:T(8,128)S(1)} %screened_spectrum.1.screened_ref, bf16[512,1024]{1,0:T(8,128)(2,1)S(1)} %get-tuple-element.72.high_ref, bf16[512,1024]{1,0:T(8,128)(2,1)S(1)} %get-tuple-element.73.low_ref, ...), custom_call_target="tpu_custom_call" | custom-call | tf_op jit(solution)/shard_map/convolve/pallas_call | solution.py:257
  99.5 17.9 %all_to_all.15.packed_ref = f32[64,8,128]{2,1,0:T(8,128)S(1)} all-to-all(f32[64,8,128]{2,1,0:T(8,128)S(1)} %convolve.1), channel_id=1, replica_groups=mesh['energy'=64,'space'=16] {'energy'}, dimensions={0} | all-to-all | bytes 524288 | tf_op jit(solution)/shard_map/all_to_all | solution.py:261
  117.4 1.1 unpack_result.1
  (21 shorter events, 0.0 us)
Async XLA Ops:
  0.0 2.2 %collective-permute-start = (f32[64,384]{1,0:T(8,128)}, f32[64,384]{1,0:T(8,128)S(1)}, u32[]{:S(2)}, u32[]{:S(2)}) collective-permute-start(f32[64,384]{1,0:T(8,128)} %bitcast.6), channel_id=1, source_target_pairs={{0,1},{16,17},{32,33},{48,49},{64,65},{80,81},{96,97},{112,113},{1... | collective-permute-start | bytes 294920 | tf_op jit(solution)/shard_map/ppermute | solution.py:272
  0.7 1.3 %copy-start.1 = (f32[2,384,384]{2,1,0:T(8,128)S(1)}, f32[2,384,384]{2,1,0:T(8,128)}, u32[]{:S(2)}) copy-start(f32[2,384,384]{2,1,0:T(8,128)} %map_ref.2) | copy-start | bytes 3538948
  1.9 0.9 copy-start.8
  3.2 0.7 collective-permute-start.1
  4.2 0.7 collective-permute-start.2
  5.2 0.7 collective-permute-start.3
  6.2 0.7 collective-permute-start.4
  7.2 0.7 collective-permute-start.5
  8.2 0.7 collective-permute-start.6
  9.2 0.7 collective-permute-start.7
  9.9 2.0 %copy-start.5 = (f32[2,1024,32]{1,2,0:T(8,128)S(1)}, f32[2,1024,32]{1,2,0:T(8,128)}, u32[]{:S(2)}) copy-start(f32[2,1024,32]{1,2,0:T(8,128)} %param.15) | copy-start | bytes 786436
  10.3 0.7 collective-permute-start.8
  11.3 12.6 %collective-permute-start.9 = (f32[64,384]{1,0:T(8,128)S(1)}, f32[64,384]{1,0:T(8,128)S(1)}, u32[]{:S(2)}, u32[]{:S(2)}) collective-permute-start(f32[64,384]{1,0:T(8,128)S(1)} %get-tuple-element.58.state_ref), channel_id=1, source_target_pairs={{9,10},{25,26},{41,42},{57,58},{73,74},{89,90},{105,106},{121,122}... | collective-permute-start | bytes 294920 | tf_op jit(solution)/shard_map/ppermute | solution.py:272
  13.0 45.0 %all-to-all-start.1 = ((f32[64,8,128]{2,1,0:T(8,128)}), f32[64,8,128]{2,1,0:T(8,128)S(1)}, u32[]{:S(2)}, u32[]{:S(2)}) async-start(f32[64,8,128]{2,1,0:T(8,128)} %pack_screened.1), calls=%async_computation.1 | async-start | bytes 524288 | tf_op jit(solution)/shard_map/all_to_all | solution.py:261
  24.2 0.7 collective-permute-start.10
  25.2 0.7 collective-permute-start.11
  26.2 0.7 collective-permute-start.12
  26.9 2.8 %copy-start = (f32[2,384,768]{2,1,0:T(8,128)S(1)}, f32[2,384,768]{2,1,0:T(8,128)}, u32[]{:S(2)}) copy-start(f32[2,384,768]{2,1,0:T(8,128)} %map_ref.3) | copy-start | bytes 7077892
  27.2 0.8 collective-permute-start.13
  28.4 1.7 %copy-start.12 = (s32[2,1024]{1,0:T(2,128)S(1)}, s32[2,1024]{1,0:T(2,128)}, u32[]{:S(2)}) copy-start(s32[2,1024]{1,0:T(2,128)} %pairs_ref.1) | copy-start | bytes 24580
  28.4 27.5 %collective-permute-start.14 = (f32[64,384]{1,0:T(8,128)S(1)}, f32[64,384]{1,0:T(8,128)S(1)}, u32[]{:S(2)}, u32[]{:S(2)}) collective-permute-start(f32[64,384]{1,0:T(8,128)S(1)} %get-tuple-element.68), channel_id=1, source_target_pairs={{14,15},{30,31},{46,47},{62,63},{78,79},{94,95},{110,111},{126,127... | collective-permute-start | bytes 294920 | tf_op jit(solution)/shard_map/ppermute | solution.py:272
  30.0 25.9 %copy-start.6 = (f32[2,768,32]{1,2,0:T(8,128)S(1)}, f32[2,768,32]{1,2,0:T(8,128)}, u32[]{:S(2)}) copy-start(f32[2,768,32]{1,2,0:T(8,128)} %param.14) | copy-start | bytes 589828
  55.9 29.7 %copy-start.7 = (f32[2,32,512]{2,1,0:T(8,128)S(1)}, f32[2,32,512]{2,1,0:T(8,128)}, u32[]{:S(2)}) copy-start(f32[2,32,512]{2,1,0:T(8,128)} %constant.13.clone.fine_ref) | copy-start | bytes 393220
  55.9 29.7 %copy-start.9 = (f32[2,16,512]{2,1,0:T(8,128)S(1)}, f32[2,16,512]{2,1,0:T(8,128)}, u32[]{:S(2)}) copy-start(f32[2,16,512]{2,1,0:T(8,128)} %constant.12.clone.coarse_ref) | copy-start | bytes 196612
  55.9 29.7 %copy-start.10 = (f32[2,32,128]{2,1,0:T(8,128)S(1)}, f32[2,32,128]{2,1,0:T(8,128)}, u32[]{:S(2)}) copy-start(f32[2,32,128]{2,1,0:T(8,128)} %constant.15.clone.inner_ref) | copy-start | bytes 98308
  55.9 29.7 %copy-start.11 = (f32[2,16,128]{2,1,0:T(8,128)S(1)}, f32[2,16,128]{2,1,0:T(8,128)}, u32[]{:S(2)}) copy-start(f32[2,16,128]{2,1,0:T(8,128)} %constant.14.clone.outer_ref) | copy-start | bytes 49156
  55.9 30.2 %copy-start.4 = (bf16[2,128,128]{2,1,0:T(8,128)(2,1)S(1)}, bf16[2,128,128]{2,1,0:T(8,128)(2,1)}, u32[]{:S(2)}) copy-start(bf16[2,128,128]{2,1,0:T(8,128)(2,1)} %constant.16.clone.lanes_ref) | copy-start | bytes 196612
  58.1 0.7 copy-start.2
  58.8 38.8 %all-to-all-start = ((f32[64,8,128]{2,1,0:T(8,128)}), f32[64,8,128]{2,1,0:T(8,128)S(1)}, u32[]{:S(2)}, u32[]{:S(2)}) async-start(f32[64,8,128]{2,1,0:T(8,128)} %packed_lesser.1), calls=%async_computation | async-start | bytes 524288 | tf_op jit(solution)/shard_map/all_to_all | solution.py:261
  86.1 1.0 copy-start.3

commit v2 on v1

--- a/solution.py
+++ b/solution.py
@@ -1,3 +1,5 @@
+import functools
+
 import jax
 import jax.numpy as jnp
 import numpy as np
@@ -6,16 +8,19 @@
 from jax.experimental.pallas import tpu as pltpu
 from jax.sharding import PartitionSpec as P
 
+
+SINGLES = 5
+LEADERS = (7, 10, 13)
+
 f32 = jnp.float32
 bf16 = jnp.bfloat16
 
 
-def call(kernel, out_shape, name, megabytes, scratch=()):
+def call(kernel, out_shape, megabytes, scratch=()):
     return pl.pallas_call(
         kernel,
         out_shape=out_shape,
         scratch_shapes=list(scratch),
-        name=name,
         compiler_params=pltpu.CompilerParams(vmem_limit_bytes=megabytes << 20),
     )
 
@@ -50,21 +55,65 @@
 
 def split_map(value):
     shape = jax.ShapeDtypeStruct((value.shape[1], 2 * value.shape[2]), bf16)
-    return call(split_kernel, [shape, shape], "split_map", 8)(value)
-
-
-def step_kernel(arrived_ref, state_ref, entering_ref, high_ref, low_ref, state_out, entering_out):
-    arrived = arrived_ref[...]
-    half = arrived.shape[0] // 2
-    entering_out[...] = entering_ref[...] + arrived
-    real, imag = complex_rows_dot(arrived, high_ref, low_ref)
-    state_out[:half] = state_ref[:half] + real
-    state_out[half:] = state_ref[half:] + imag
-
-
-def chain_step(arrived, state, entering, high, low):
-    shape = jax.ShapeDtypeStruct(state.shape, f32)
-    return call(step_kernel, [shape, shape], "chain_step", 6)(arrived, state, entering, high, low)
+    return call(split_kernel, [shape, shape], 8)(value)
+
+
+def advanced(state, high_ref, low_ref, source_ref):
+    real, imag = complex_rows_dot(state, high_ref, low_ref)
+    return jnp.concatenate([real, imag], axis=0) + source_ref[...]
+
+
+def first_kernel(number, place_ref, arrived_ref, *refs):
+    operands, (entering_ref, middle_ref, state_ref) = refs[:3], refs[3:]
+    middle_ref[...] = jnp.zeros_like(middle_ref)
+
+    @pl.when(place_ref[0] == number)
+    def _():
+        arrived = arrived_ref[...]
+        entering_ref[...] = arrived
+        state_ref[...] = advanced(arrived, *operands)
+
+    @pl.when(place_ref[0] != number)
+    def _():
+        entering_ref[...] = jnp.zeros_like(entering_ref)
+        state_ref[...] = jnp.zeros_like(state_ref)
+
+
+def single_kernel(number, place_ref, arrived_ref, *refs):
+    operands, (entering_ref, state_ref) = refs[:3], refs[5:]
+
+    @pl.when(place_ref[0] == number)
+    def _():
+        arrived = arrived_ref[...]
+        entering_ref[...] = arrived
+        state_ref[...] = advanced(arrived, *operands)
+
+
+def triple_kernel(number, place_ref, arrived_ref, *refs):
+    before, own, after = refs[0:3], refs[3:6], refs[6:9]
+    entering_ref, middle_ref, state_ref = refs[12:]
+
+    @pl.when(place_ref[0] == number)
+    def _():
+        first = advanced(arrived_ref[...], *before)
+        entering_ref[...] = first
+        second = advanced(first, *own)
+        middle_ref[...] = second
+        state_ref[...] = advanced(second, *after)
+
+
+def on_plane(kernel, number, place, operands, held, fresh=()):
+    vmem = pl.BlockSpec(memory_space=pltpu.VMEM)
+    count = 1 + len(operands)
+    results = (*held, *fresh)
+    return pl.pallas_call(
+        functools.partial(kernel, number),
+        out_shape=[jax.ShapeDtypeStruct(value.shape, value.dtype) for value in results],
+        in_specs=[pl.BlockSpec(memory_space=pltpu.SMEM)] + [vmem] * (len(operands) + len(held)),
+        out_specs=[vmem] * len(results),
+        input_output_aliases={count + index: index for index in range(len(held))},
+        compiler_params=pltpu.CompilerParams(vmem_limit_bytes=6 << 20),
+    )(place, *operands, *held)
 
 
 def swap_blocks(parts):
@@ -107,12 +156,12 @@
 
 def pack_array(values):
     shape = jax.ShapeDtypeStruct((64, 8, 128), f32)
-    return call(pack_kernel, shape, "pack_screened", 4, [pltpu.VMEM((2, 8, 32, 128), f32)])(values)
+    return call(pack_kernel, shape, 4, [pltpu.VMEM((2, 8, 32, 128), f32)])(values)
 
 
 def unpack_array(packed):
     shape = jax.ShapeDtypeStruct((2, 32, 1024), f32)
-    return call(unpack_kernel, shape, "unpack_result", 4, [pltpu.VMEM((2, 8, 32, 128), f32)])(packed)
+    return call(unpack_kernel, shape, 4, [pltpu.VMEM((2, 8, 32, 128), f32)])(packed)
 
 
 def choose_kernel(pairs_ref, chosen_ref):
@@ -127,13 +176,13 @@
 
 def choose(pairs, orbitals):
     shape = jax.ShapeDtypeStruct((orbitals, 2 * pairs.shape[1]), bf16)
-    return call(choose_kernel, shape, "choose", 8)(pairs)
+    return call(choose_kernel, shape, 8)(pairs)
 
 
 def lesser_kernel(
-    arrived_ref, entering_ref, high_ref, low_ref, source_ref, chosen_ref, packed_ref, stage_ref
+    arrived_ref, other_ref, entering_ref, high_ref, low_ref, source_ref, chosen_ref, packed_ref, stage_ref
 ):
-    state = entering_ref[...] + arrived_ref[...]
+    state = entering_ref[...] + (arrived_ref[...] + other_ref[...])
     real, imag = complex_rows_dot(state, high_ref, low_ref)
     wave = jnp.concatenate([real + source_ref[0], imag + source_ref[1]], axis=0)
     rows, half = wave.shape[0], wave.shape[0] // 2
@@ -151,11 +200,11 @@
     pack(stage_ref, packed_ref)
 
 
-def packed_lesser(arrived, entering, high, low, source, chosen):
+def packed_lesser(arrived, other, entering, high, low, source, chosen):
     shape = jax.ShapeDtypeStruct((64, 8, 128), f32)
     scratch = [pltpu.VMEM((2, 8, 32, 128), f32)]
-    return call(lesser_kernel, shape, "packed_lesser", 14, scratch)(
-        arrived, entering, high, low, source, chosen
+    return call(lesser_kernel, shape, 14, scratch)(
+        arrived, other, entering, high, low, source, chosen
     )
 
 
@@ -203,7 +252,7 @@
     *small, lanes = small_tables()
     waves = jax.ShapeDtypeStruct((512, 1024), bf16)
     shapes = [waves, waves, jax.ShapeDtypeStruct((2, 512, 128), f32)]
-    return (*call(tables_kernel, shapes, "tables", 8)(*small), lanes)
+    return (*call(tables_kernel, shapes, 8)(*small), lanes)
 
 
 def turned(value):
@@ -249,12 +298,12 @@
 
 def screened_spectrum(packed, constants):
     shape = jax.ShapeDtypeStruct((2, 512, 128), f32)
-    return call(screened_kernel, shape, "screened_spectrum", 8)(packed, *constants)
+    return call(screened_kernel, shape, 8)(packed, *constants)
 
 
 def convolve(packed, screened, constants):
     shape = jax.ShapeDtypeStruct((64, 8, 128), f32)
-    return call(convolve_kernel, shape, "convolve", 8)(packed, screened, *constants)
+    return call(convolve_kernel, shape, 8)(packed, screened, *constants)
 
 
 def exchange(packed):
@@ -263,21 +312,43 @@
 
 def body(chain_map, chain_source, local_map, local_source, interaction, element_pairs):
     constants = tables()
-    partitions = lax.axis_size("space")
+    place = lax.axis_index("space").astype(jnp.int32).reshape(1)
     rows = 2 * chain_source.shape[1]
-    state = chain_source.reshape(rows, chain_source.shape[2])
-    entering = jnp.zeros_like(state)
-    map_high, map_low = split_map(chain_map)
-    for place in range(1, partitions):
-        arrived = lax.ppermute(state, "space", [(place - 1, place)])
-        if place < partitions - 1:
-            state, entering = chain_step(arrived, state, entering, map_high, map_low)
+    source = chain_source.reshape(rows, chain_source.shape[2])
+
+    def move(value, *pairs):
+        return lax.ppermute(value, "space", pairs)
+
+    arrived = move(source, (0, 1))
+    upward = [(leader - 1, leader) for leader in LEADERS]
+    downward = [(leader + 1, leader) for leader in LEADERS]
+    before = (move(chain_map, *upward), move(source, *upward))
+    after = (move(chain_map, *downward), move(source, *downward))
+    own = (*split_map(chain_map), source)
+    entering, middle, state = on_plane(first_kernel, 1, place, (arrived, *own), (), (source,) * 3)
+    for number in range(2, SINGLES + 1):
+        arrived = move(state, (number - 1, number))
+        entering, state = on_plane(
+            single_kernel, number, place, (arrived, *own), (entering, state)
+        )
+    before = (*split_map(before[0]), before[1])
+    after = (*split_map(after[0]), after[1])
+    last = SINGLES
+    for leader in LEADERS:
+        arrived = move(state, (last, leader))
+        operands = (arrived, *before, *own, *after)
+        entering, middle, state = on_plane(
+            triple_kernel, leader, place, operands, (entering, middle, state)
+        )
+        last = leader
+    arrived = move(state, (SINGLES, SINGLES + 1), *((leader, leader + 2) for leader in LEADERS))
+    other = move(middle, *((leader, leader + 1) for leader in LEADERS))
     screened = exchange(pack_array(jnp.swapaxes(interaction, 1, 2)))
     screened = screened_spectrum(screened, constants)
     local_high, local_low = split_map(local_map)
     chosen = choose(element_pairs, local_map.shape[2])
-    source = jnp.swapaxes(local_source, 1, 2)
-    packed = packed_lesser(arrived, entering, local_high, local_low, source, chosen)
+    constant = jnp.swapaxes(local_source, 1, 2)
+    packed = packed_lesser(arrived, other, entering, local_high, local_low, constant, chosen)
     result = convolve(exchange(packed), screened, constants)
     return jnp.swapaxes(unpack_array(exchange(result)), 1, 2)
 
@@ -292,4 +363,5 @@
         P(None, "space"),
     )
     out_specs = P(None, "space", "energy")
+
     return jax.shard_map(body, mesh=mesh, in_specs=in_specs, out_specs=out_specs, check_vma=False)

time: 119 us -> 104 us (0.87)
  the two profiles are of different devices: /device:TPU:961 before, /device:TPU:897 now
where the time goes in v2:
time: 104 us; the launch traced here: 103 us
  starting transfers between devices  39.9 us (38%)
  waiting for transfers between devices  31.2 us (30%)
  blocking collectives  17.8 us (17%)
  Pallas kernels  11.3 us (11%)
  local copies, waits for them, and re-layouts  2.26 us (2%)
    all_to_all x2, starting transfers between devices, exchange(): lax.all_to_all(packed, 'energy', split_axis=0, concat_axis=0, tiled=True)  26.5 us
    ppermute x14, waiting for transfers between devices, move(): return lax.ppermute(value, 'space', pairs)  22 us
    all_to_all x1, blocking collectives, exchange(): lax.all_to_all(packed, 'energy', split_axis=0, concat_axis=0, tiled=True)  17.8 us
    ppermute x14, starting transfers between devices, move(): return lax.ppermute(value, 'space', pairs)  13.5 us
    all_to_all x2, waiting for transfers between devices, exchange(): lax.all_to_all(packed, 'energy', split_axis=0, concat_axis=0, tiled=True)  9.28 us
    pallas_call x4, Pallas kernels, split_map(): return call(split_kernel, [shape, shape], 8)(value)  2.27 us
    unnamed x26, local copies, waits for them, and re-layouts  2.26 us
    pallas_call x1, Pallas kernels, packed_lesser(): call(lesser_kernel, shape, 14, scratch)  2.15 us
  transfers between devices with their start and end apart: 16, of which 4 were waited for; matrix products, arithmetic and copies ran while one was open for 0% of the time, Pallas kernels for 8%

profile of v2, /device:TPU:897, one launch (start us, length us, event | category | flops | bytes accessed | tf_op | source)
XLA Modules:
  0.0 103.0 jit_solution(701652666858060041)
XLA Ops:
  0.0 1.8 %collective-permute-start.6 = (f32[2,384,384]{2,1,0:T(8,128)}, f32[2,384,384]{2,1,0:T(8,128)}, u32[]{:S(2)}, u32[]{:S(2)}) collective-permute-start(f32[2,384,384]{2,1,0:T(8,128)} %map_ref.2), channel_id=1, source_target_pairs={{6,7},{9,10},{12,13},{22,23},{25,26},{28,29},{38,39},{41,42},{44,4... | collective-permute-start | bytes 3538952 | tf_op jit(solution)/shard_map/ppermute | solution.py:320
  1.8 1.8 %collective-permute-start.8 = (f32[2,384,384]{2,1,0:T(8,128)}, f32[2,384,384]{2,1,0:T(8,128)S(1)}, u32[]{:S(2)}, u32[]{:S(2)}) collective-permute-start(f32[2,384,384]{2,1,0:T(8,128)} %map_ref.2), channel_id=1, source_target_pairs={{8,7},{11,10},{14,13},{24,23},{27,26},{30,29},{40,39},{43,42},{46,... | collective-permute-start | bytes 3538952 | tf_op jit(solution)/shard_map/ppermute | solution.py:320
  3.7 0.7 collective-permute-start
  4.4 0.0 copy-start.2
  4.4 1.3 %copy-done.2 = f32[2,384,384]{2,1,0:T(8,128)S(1)} copy-done((f32[2,384,384]{2,1,0:T(8,128)S(1)}, f32[2,384,384]{2,1,0:T(8,128)}, u32[]{:S(2)}) %copy-start.2) | copy-done | bytes 1179672
  5.6 0.2 shard_map.109
  5.9 0.0 collective-permute-done.arrived_ref
  5.9 0.0 copy-done
  5.9 0.7 collective-permute-start.1
  6.6 0.0 collective-permute-done.1.arrived_ref
  6.6 0.0 copy-start.6
  6.6 0.8 collective-permute-start.2
  7.4 0.0 collective-permute-done.2.arrived_ref
  7.5 0.7 collective-permute-start.3
  8.1 0.0 copy-done.6
  8.2 1.1 %shard_map.123 = f32[64,8,128]{2,1,0:T(8,128)} custom-call(f32[2,32,1024]{2,1,0:T(8,128)S(1)} %bitcast.16), custom_call_target="tpu_custom_call" | custom-call | tf_op jit(solution)/shard_map/pallas_call | solution.py:159
  9.2 11.1 %all-to-all-start.1 = ((f32[64,8,128]{2,1,0:T(8,128)}), f32[64,8,128]{2,1,0:T(8,128)S(1)}, u32[]{:S(2)}, u32[]{:S(2)}) async-start(f32[64,8,128]{2,1,0:T(8,128)} %shard_map.123), calls=%async_computation.1 | async-start | bytes 524288 | tf_op jit(solution)/shard_map/all_to_all | solution.py:310
  20.3 0.0 collective-permute-done.3.arrived_ref
  20.3 0.7 collective-permute-start.4
  21.0 0.7 collective-permute-start.7
  21.7 1.6 %collective-permute-start.9 = (f32[64,384]{1,0:T(8,128)S(1)}, f32[64,384]{1,0:T(8,128)S(1)}, u32[]{:S(2)}, u32[]{:S(2)}) collective-permute-start(f32[64,384]{1,0:T(8,128)S(1)} %bitcast.11), channel_id=1, source_target_pairs={{8,7},{11,10},{14,13},{24,23},{27,26},{30,29},{40,39},{43,42},{46,... | collective-permute-start | bytes 294920 | tf_op jit(solution)/shard_map/ppermute | solution.py:320
  23.3 0.0 collective-permute-done.4.arrived_ref
  23.3 0.7 collective-permute-start.5
  24.0 0.0 collective-permute-done.6.map_ref
  24.0 1.5 %shard_map.115 = (bf16[384,768]{1,0:T(8,128)(2,1)S(1)}, bf16[384,768]{1,0:T(8,128)(2,1)S(1)}) custom-call(f32[2,384,384]{2,1,0:T(8,128)} %collective-permute-done.6.map_ref), custom_call_target="tpu_custom_call" | custom-call | tf_op jit(solution)/shard_map/pallas_call | solution.py:58
  25.5 3.1 %collective-permute-done.8.map_ref = f32[2,384,384]{2,1,0:T(8,128)S(1)} collective-permute-done((f32[2,384,384]{2,1,0:T(8,128)}, f32[2,384,384]{2,1,0:T(8,128)S(1)}, u32[]{:S(2)}, u32[]{:S(2)}) %collective-permute-start.8) | collective-permute-done | bytes 1179680 | tf_op jit(solution)/shard_map/ppermute | solution.py:320
  28.6 0.2 shard_map.116
  28.8 0.0 collective-permute-done.7.refs_2_
  28.8 1.8 %collective-permute-done.9.refs_8_ = f32[64,384]{1,0:T(8,128)S(1)} collective-permute-done((f32[64,384]{1,0:T(8,128)S(1)}, f32[64,384]{1,0:T(8,128)S(1)}, u32[]{:S(2)}, u32[]{:S(2)}) %collective-permute-start.9) | collective-permute-done | bytes 98336 | tf_op jit(solution)/shard_map/ppermute | solution.py:320
  30.6 0.0 collective-permute-done.5.arrived_ref
  30.6 0.7 collective-permute-start.10
  31.2 0.0 collective-permute-done.10.arrived_ref
  31.3 0.7 collective-permute-start.11
  31.9 0.0 collective-permute-done.11.arrived_ref
  31.9 0.0 copy-start.1
  32.0 0.8 collective-permute-start.12
  32.8 0.0 copy-start.12
  32.8 1.3 %collective-permute-start.13 = (f32[64,384]{1,0:T(8,128)S(1)}, f32[64,384]{1,0:T(8,128)S(1)}, u32[]{:S(2)}, u32[]{:S(2)}) collective-permute-start(f32[64,384]{1,0:T(8,128)S(1)} %get-tuple-element.60), channel_id=1, source_target_pairs={{7,8},{10,11},{13,14},{23,24},{26,27},{29,30},{39,40},{42,43},{45,... | collective-permute-start | bytes 294920 | tf_op jit(solution)/shard_map/ppermute | solution.py:320
  34.1 0.0 copy-done.1
  34.1 0.3 shard_map.120
  34.4 0.0 copy-done.12
  34.4 0.0 copy-start.7
  34.5 1.0 shard_map.121.chosen_ref
  35.4 0.0 collective-permute-done.12.arrived_ref
  35.4 17.1 %collective-permute-done.13.other_ref = f32[64,384]{1,0:T(8,128)S(1)} collective-permute-done((f32[64,384]{1,0:T(8,128)S(1)}, f32[64,384]{1,0:T(8,128)S(1)}, u32[]{:S(2)}, u32[]{:S(2)}) %collective-permute-start.13) | collective-permute-done | bytes 98336 | tf_op jit(solution)/shard_map/ppermute | solution.py:320
  52.5 0.0 copy-done.7
  52.5 0.0 copy-start.11
  52.6 0.0 copy-start.5
  52.6 2.1 %shard_map.122 = f32[64,8,128]{2,1,0:T(8,128)} custom-call(f32[64,384]{1,0:T(8,128)S(1)} %collective-permute-done.12.arrived_ref, f32[64,384]{1,0:T(8,128)S(1)} %collective-permute-done.13.other_ref, f32[64,384]{1,0:T(8,128)S(1)} %get-tuple-element.61.entering_ref, bf16[384,1536]{1,0:T(8,128)(2,1)S(1)} %get-tuple-element.62.high_ref, ...), custom_call_target="tpu_custom_call" | custom-call | tf_op jit(solution)/shard_map/pallas_call | solution.py:206
  54.7 0.0 all-to-all-done.1.packed_ref
  54.7 15.4 %all-to-all-start = ((f32[64,8,128]{2,1,0:T(8,128)}), f32[64,8,128]{2,1,0:T(8,128)S(1)}, u32[]{:S(2)}, u32[]{:S(2)}) async-start(f32[64,8,128]{2,1,0:T(8,128)} %shard_map.122), calls=%async_computation | async-start | bytes 524288 | tf_op jit(solution)/shard_map/all_to_all | solution.py:310
  70.1 0.0 copy-done.8
  70.2 0.0 copy-done.9
  70.2 0.0 copy-done.10
  70.2 0.0 copy-done.11
  70.2 0.5 shard_map.124
  70.7 0.0 copy-done.3
  70.7 0.0 copy-done.5
  70.8 0.9 copy-done.4
  71.7 1.1 %shard_map.125.screened_ref = f32[2,512,128]{2,1,0:T(8,128)S(1)} custom-call(f32[64,8,128]{2,1,0:T(8,128)S(1)} %copy-done.4, bf16[512,1024]{1,0:T(8,128)(2,1)S(1)} %get-tuple-element.64.high_ref, bf16[512,1024]{1,0:T(8,128)(2,1)S(1)} %get-tuple-element.65.low_ref, f32[2,512,128]{2,1,0:T(8,128)S(1)} %get-tuple-element.66.twiddle_ref, ...), custom_call_target="tpu_custom_call" | custom-call | tf_op jit(solution)/shard_map/pallas_call | solution.py:301
  72.8 9.3 %all-to-all-done.packed_ref = f32[64,8,128]{2,1,0:T(8,128)S(1)} async-done(((f32[64,8,128]{2,1,0:T(8,128)}), f32[64,8,128]{2,1,0:T(8,128)S(1)}, u32[]{:S(2)}, u32[]{:S(2)}) %all-to-all-start) | async-done | bytes 262176 | tf_op jit(solution)/shard_map/all_to_all | solution.py:310
  82.1 2.0 %shard_map.126 = f32[64,8,128]{2,1,0:T(8,128)S(1)} custom-call(f32[64,8,128]{2,1,0:T(8,128)S(1)} %all-to-all-done.packed_ref, f32[2,512,128]{2,1,0:T(8,128)S(1)} %shard_map.125.screened_ref, bf16[512,1024]{1,0:T(8,128)(2,1)S(1)} %get-tuple-element.64.high_ref, bf16[512,1024]{1,0:T(8,128)(2,1)S(1)} %get-tuple-element.65.low_ref, ...), custom_call_target="tpu_custom_call" | custom-call | tf_op jit(solution)/shard_map/pallas_call | solution.py:306
  84.1 17.8 %all_to_all.15.packed_ref = f32[64,8,128]{2,1,0:T(8,128)S(1)} all-to-all(f32[64,8,128]{2,1,0:T(8,128)S(1)} %shard_map.126), channel_id=1, replica_groups=mesh['energy'=64,'space'=16] {'energy'}, dimensions={0} | all-to-all | bytes 524288 | tf_op jit(solution)/shard_map/all_to_all | solution.py:310
  101.9 1.1 %shard_map.127 = f32[2,32,1024]{2,1,0:T(8,128)} custom-call(f32[64,8,128]{2,1,0:T(8,128)S(1)} %all_to_all.15.packed_ref), custom_call_target="tpu_custom_call" | custom-call | tf_op jit(solution)/shard_map/pallas_call | solution.py:164
  (14 shorter events, 0.1 us)
Async XLA Ops:
  0.0 5.9 %copy-start = (f32[2,32,384]{2,1,0:T(8,128)S(1)}, f32[2,32,384]{2,1,0:T(8,128)}, u32[]{:S(2)}) copy-start(f32[2,32,384]{2,1,0:T(8,128)} %param.12) | copy-start | bytes 294916
  0.0 24.0 %collective-permute-start.6 = (f32[2,384,384]{2,1,0:T(8,128)}, f32[2,384,384]{2,1,0:T(8,128)}, u32[]{:S(2)}, u32[]{:S(2)}) collective-permute-start(f32[2,384,384]{2,1,0:T(8,128)} %map_ref.2), channel_id=1, source_target_pairs={{6,7},{9,10},{12,13},{22,23},{25,26},{28,29},{38,39},{41,42},{44,4... | collective-permute-start | bytes 3538952 | tf_op jit(solution)/shard_map/ppermute | solution.py:320
  1.8 26.7 %collective-permute-start.8 = (f32[2,384,384]{2,1,0:T(8,128)}, f32[2,384,384]{2,1,0:T(8,128)S(1)}, u32[]{:S(2)}, u32[]{:S(2)}) collective-permute-start(f32[2,384,384]{2,1,0:T(8,128)} %map_ref.2), channel_id=1, source_target_pairs={{8,7},{11,10},{14,13},{24,23},{27,26},{30,29},{40,39},{43,42},{46,... | collective-permute-start | bytes 3538952 | tf_op jit(solution)/shard_map/ppermute | solution.py:320
  3.7 2.2 %collective-permute-start = (f32[64,384]{1,0:T(8,128)}, f32[64,384]{1,0:T(8,128)S(1)}, u32[]{:S(2)}, u32[]{:S(2)}) collective-permute-start(f32[64,384]{1,0:T(8,128)} %bitcast.5), channel_id=1, source_target_pairs={{0,1},{16,17},{32,33},{48,49},{64,65},{80,81},{96,97},{112,113},{1... | collective-permute-start | bytes 294920 | tf_op jit(solution)/shard_map/ppermute | solution.py:320
  4.4 1.3 %copy-start.2 = (f32[2,384,384]{2,1,0:T(8,128)S(1)}, f32[2,384,384]{2,1,0:T(8,128)}, u32[]{:S(2)}) copy-start(f32[2,384,384]{2,1,0:T(8,128)} %map_ref.2) | copy-start | bytes 3538948
  5.9 0.7 collective-permute-start.1
  6.6 1.5 %copy-start.6 = (f32[2,1024,32]{1,2,0:T(8,128)S(1)}, f32[2,1024,32]{1,2,0:T(8,128)}, u32[]{:S(2)}) copy-start(f32[2,1024,32]{1,2,0:T(8,128)} %param.15) | copy-start | bytes 786436
  6.6 0.8 collective-permute-start.2
  7.5 12.9 %collective-permute-start.3 = (f32[64,384]{1,0:T(8,128)S(1)}, f32[64,384]{1,0:T(8,128)S(1)}, u32[]{:S(2)}, u32[]{:S(2)}) collective-permute-start(f32[64,384]{1,0:T(8,128)S(1)} %get-tuple-element.42.refs_4_), channel_id=1, source_target_pairs={{3,4},{19,20},{35,36},{51,52},{67,68},{83,84},{99,100},{115,116},{... | collective-permute-start | bytes 294920 | tf_op jit(solution)/shard_map/ppermute | solution.py:320
  9.2 45.5 %all-to-all-start.1 = ((f32[64,8,128]{2,1,0:T(8,128)}), f32[64,8,128]{2,1,0:T(8,128)S(1)}, u32[]{:S(2)}, u32[]{:S(2)}) async-start(f32[64,8,128]{2,1,0:T(8,128)} %shard_map.123), calls=%async_computation.1 | async-start | bytes 524288 | tf_op jit(solution)/shard_map/all_to_all | solution.py:310
  20.3 2.9 %collective-permute-start.4 = (f32[64,384]{1,0:T(8,128)S(1)}, f32[64,384]{1,0:T(8,128)S(1)}, u32[]{:S(2)}, u32[]{:S(2)}) collective-permute-start(f32[64,384]{1,0:T(8,128)S(1)} %get-tuple-element.44.refs_4_), channel_id=1, source_target_pairs={{4,5},{20,21},{36,37},{52,53},{68,69},{84,85},{100,101},{116,117},... | collective-permute-start | bytes 294920 | tf_op jit(solution)/shard_map/ppermute | solution.py:320
  21.0 7.8 %collective-permute-start.7 = (f32[64,384]{1,0:T(8,128)S(1)}, f32[64,384]{1,0:T(8,128)S(1)}, u32[]{:S(2)}, u32[]{:S(2)}) collective-permute-start(f32[64,384]{1,0:T(8,128)S(1)} %bitcast.10), channel_id=1, source_target_pairs={{6,7},{9,10},{12,13},{22,23},{25,26},{28,29},{38,39},{41,42},{44,4... | collective-permute-start | bytes 294920 | tf_op jit(solution)/shard_map/ppermute | solution.py:320
  21.7 8.9 %collective-permute-start.9 = (f32[64,384]{1,0:T(8,128)S(1)}, f32[64,384]{1,0:T(8,128)S(1)}, u32[]{:S(2)}, u32[]{:S(2)}) collective-permute-start(f32[64,384]{1,0:T(8,128)S(1)} %bitcast.11), channel_id=1, source_target_pairs={{8,7},{11,10},{14,13},{24,23},{27,26},{30,29},{40,39},{43,42},{46,... | collective-permute-start | bytes 294920 | tf_op jit(solution)/shard_map/ppermute | solution.py:320
  23.3 7.3 %collective-permute-start.5 = (f32[64,384]{1,0:T(8,128)S(1)}, f32[64,384]{1,0:T(8,128)S(1)}, u32[]{:S(2)}, u32[]{:S(2)}) collective-permute-start(f32[64,384]{1,0:T(8,128)S(1)} %get-tuple-element.46.refs_11_), channel_id=1, source_target_pairs={{5,7},{21,23},{37,39},{53,55},{69,71},{85,87},{101,103},{117,119},... | collective-permute-start | bytes 294920 | tf_op jit(solution)/shard_map/ppermute | solution.py:320
  30.6 0.7 collective-permute-start.10
  31.3 0.7 collective-permute-start.11
  31.9 2.2 %copy-start.1 = (f32[2,384,768]{2,1,0:T(8,128)S(1)}, f32[2,384,768]{2,1,0:T(8,128)}, u32[]{:S(2)}) copy-start(f32[2,384,768]{2,1,0:T(8,128)} %map_ref.3) | copy-start | bytes 7077892
  32.0 3.4 %collective-permute-start.12 = (f32[64,384]{1,0:T(8,128)S(1)}, f32[64,384]{1,0:T(8,128)S(1)}, u32[]{:S(2)}, u32[]{:S(2)}) collective-permute-start(f32[64,384]{1,0:T(8,128)S(1)} %get-tuple-element.59), channel_id=1, source_target_pairs={{5,6},{7,9},{10,12},{13,15},{21,22},{23,25},{26,28},{29,31},{37,38... | collective-permute-start | bytes 294920 | tf_op jit(solution)/shard_map/ppermute | solution.py:320
  32.8 1.7 %copy-start.12 = (s32[2,1024]{1,0:T(2,128)S(1)}, s32[2,1024]{1,0:T(2,128)}, u32[]{:S(2)}) copy-start(s32[2,1024]{1,0:T(2,128)} %pairs_ref.1) | copy-start | bytes 24580
  32.8 19.7 %collective-permute-start.13 = (f32[64,384]{1,0:T(8,128)S(1)}, f32[64,384]{1,0:T(8,128)S(1)}, u32[]{:S(2)}, u32[]{:S(2)}) collective-permute-start(f32[64,384]{1,0:T(8,128)S(1)} %get-tuple-element.60), channel_id=1, source_target_pairs={{7,8},{10,11},{13,14},{23,24},{26,27},{29,30},{39,40},{42,43},{45,... | collective-permute-start | bytes 294920 | tf_op jit(solution)/shard_map/ppermute | solution.py:320
  34.4 18.1 %copy-start.7 = (f32[2,768,32]{1,2,0:T(8,128)S(1)}, f32[2,768,32]{1,2,0:T(8,128)}, u32[]{:S(2)}) copy-start(f32[2,768,32]{1,2,0:T(8,128)} %param.14) | copy-start | bytes 589828
  52.5 17.6 %copy-start.8 = (f32[2,32,512]{2,1,0:T(8,128)S(1)}, f32[2,32,512]{2,1,0:T(8,128)}, u32[]{:S(2)}) copy-start(f32[2,32,512]{2,1,0:T(8,128)} %constant.15.clone.fine_ref) | copy-start | bytes 393220
  52.5 17.6 %copy-start.9 = (f32[2,16,512]{2,1,0:T(8,128)S(1)}, f32[2,16,512]{2,1,0:T(8,128)}, u32[]{:S(2)}) copy-start(f32[2,16,512]{2,1,0:T(8,128)} %constant.14.clone.coarse_ref) | copy-start | bytes 196612
  52.5 17.6 %copy-start.10 = (f32[2,32,128]{2,1,0:T(8,128)S(1)}, f32[2,32,128]{2,1,0:T(8,128)}, u32[]{:S(2)}) copy-start(f32[2,32,128]{2,1,0:T(8,128)} %constant.17.clone.inner_ref) | copy-start | bytes 98308
  52.5 17.6 %copy-start.11 = (f32[2,16,128]{2,1,0:T(8,128)S(1)}, f32[2,16,128]{2,1,0:T(8,128)}, u32[]{:S(2)}) copy-start(f32[2,16,128]{2,1,0:T(8,128)} %constant.16.clone.outer_ref) | copy-start | bytes 49156
  52.6 18.2 %copy-start.5 = (bf16[2,128,128]{2,1,0:T(8,128)(2,1)S(1)}, bf16[2,128,128]{2,1,0:T(8,128)(2,1)}, u32[]{:S(2)}) copy-start(bf16[2,128,128]{2,1,0:T(8,128)(2,1)} %constant.18.clone.lanes_ref) | copy-start | bytes 196612
  54.7 16.0 %copy-start.3 = (f32[64,8,128]{2,1,0:T(8,128)}, f32[64,8,128]{2,1,0:T(8,128)S(1)}, u32[]{:S(2)}) copy-start(f32[64,8,128]{2,1,0:T(8,128)S(1)} %all-to-all-done.1.packed_ref) | copy-start | bytes 786436
  54.7 27.4 %all-to-all-start = ((f32[64,8,128]{2,1,0:T(8,128)}), f32[64,8,128]{2,1,0:T(8,128)S(1)}, u32[]{:S(2)}, u32[]{:S(2)}) async-start(f32[64,8,128]{2,1,0:T(8,128)} %shard_map.122), calls=%async_computation | async-start | bytes 524288 | tf_op jit(solution)/shard_map/all_to_all | solution.py:310
  70.7 1.0 copy-start.4

commit v3 on v2

--- a/solution.py
+++ b/solution.py
@@ -16,7 +16,25 @@
 bf16 = jnp.bfloat16
 
 
-def call(kernel, out_shape, megabytes, scratch=()):
+def call(kernel, out_shape, megabytes, scratch=(), awaits=False):
+    if awaits:
+        vmem = pl.BlockSpec(memory_space=pltpu.VMEM)
+
+        def after(*operands):
+            specs = [vmem] * (len(operands) - 1) + [pl.BlockSpec(memory_space=pl.ANY)]
+            count = len(operands) - 1
+
+            def body(*refs):
+                kernel(*refs[:count], *refs[count + 1 :])
+
+            return pl.pallas_call(
+                body,
+                out_shape=out_shape,
+                in_specs=specs,
+                compiler_params=pltpu.CompilerParams(vmem_limit_bytes=megabytes << 20),
+            )(*operands)
+
+        return after
     return pl.pallas_call(
         kernel,
         out_shape=out_shape,
@@ -53,9 +71,9 @@
         low_ref[:, part * width : (part + 1) * width] = low
 
 
-def split_map(value):
+def split_map(value, *awaited):
     shape = jax.ShapeDtypeStruct((value.shape[1], 2 * value.shape[2]), bf16)
-    return call(split_kernel, [shape, shape], 8)(value)
+    return call(split_kernel, [shape, shape], 8, (), bool(awaited))(value, *awaited)
 
 
 def advanced(state, high_ref, low_ref, source_ref):
@@ -80,7 +98,7 @@
 
 
 def single_kernel(number, place_ref, arrived_ref, *refs):
-    operands, (entering_ref, state_ref) = refs[:3], refs[5:]
+    operands, held, (entering_ref, state_ref) = refs[:3], refs[3:5], refs[5:]
 
     @pl.when(place_ref[0] == number)
     def _():
@@ -88,10 +106,15 @@
         entering_ref[...] = arrived
         state_ref[...] = advanced(arrived, *operands)
 
+    @pl.when(place_ref[0] != number)
+    def _():
+        for before_ref, after_ref in zip(held, (entering_ref, state_ref)):
+            after_ref[...] = before_ref[...]
+
 
 def triple_kernel(number, place_ref, arrived_ref, *refs):
     before, own, after = refs[0:3], refs[3:6], refs[6:9]
-    entering_ref, middle_ref, state_ref = refs[12:]
+    held, (entering_ref, middle_ref, state_ref) = refs[9:12], refs[12:]
 
     @pl.when(place_ref[0] == number)
     def _():
@@ -101,17 +124,20 @@
         middle_ref[...] = second
         state_ref[...] = advanced(second, *after)
 
+    @pl.when(place_ref[0] != number)
+    def _():
+        for before_ref, after_ref in zip(held, (entering_ref, middle_ref, state_ref)):
+            after_ref[...] = before_ref[...]
+
 
 def on_plane(kernel, number, place, operands, held, fresh=()):
     vmem = pl.BlockSpec(memory_space=pltpu.VMEM)
-    count = 1 + len(operands)
     results = (*held, *fresh)
     return pl.pallas_call(
         functools.partial(kernel, number),
         out_shape=[jax.ShapeDtypeStruct(value.shape, value.dtype) for value in results],
         in_specs=[pl.BlockSpec(memory_space=pltpu.SMEM)] + [vmem] * (len(operands) + len(held)),
         out_specs=[vmem] * len(results),
-        input_output_aliases={count + index: index for index in range(len(held))},
         compiler_params=pltpu.CompilerParams(vmem_limit_bytes=6 << 20),
     )(place, *operands, *held)
 
@@ -248,11 +274,11 @@
         twiddle_ref[1, rows] = jnp.where(lane < 64, turn, -turn)
 
 
-def tables():
+def tables(awaited):
     *small, lanes = small_tables()
     waves = jax.ShapeDtypeStruct((512, 1024), bf16)
     shapes = [waves, waves, jax.ShapeDtypeStruct((2, 512, 128), f32)]
-    return (*call(tables_kernel, shapes, 8)(*small), lanes)
+    return (*call(tables_kernel, shapes, 8, (), True)(*small, awaited), lanes)
 
 
 def turned(value):
@@ -311,7 +337,6 @@
 
 
 def body(chain_map, chain_source, local_map, local_source, interaction, element_pairs):
-    constants = tables()
     place = lax.axis_index("space").astype(jnp.int32).reshape(1)
     rows = 2 * chain_source.shape[1]
     source = chain_source.reshape(rows, chain_source.shape[2])
@@ -331,8 +356,11 @@
         entering, state = on_plane(
             single_kernel, number, place, (arrived, *own), (entering, state)
         )
-    before = (*split_map(before[0]), before[1])
-    after = (*split_map(after[0]), after[1])
+    screened = exchange(pack_array(jnp.swapaxes(interaction, 1, 2)))
+    constants = tables(screened)
+    screened = screened_spectrum(screened, constants)
+    before = (*split_map(before[0], screened), before[1])
+    after = (*split_map(after[0], screened), after[1])
     last = SINGLES
     for leader in LEADERS:
         arrived = move(state, (last, leader))
@@ -343,8 +371,6 @@
         last = leader
     arrived = move(state, (SINGLES, SINGLES + 1), *((leader, leader + 2) for leader in LEADERS))
     other = move(middle, *((leader, leader + 1) for leader in LEADERS))
-    screened = exchange(pack_array(jnp.swapaxes(interaction, 1, 2)))
-    screened = screened_spectrum(screened, constants)
     local_high, local_low = split_map(local_map)
     chosen = choose(element_pairs, local_map.shape[2])
     constant = jnp.swapaxes(local_source, 1, 2)

time: 104 us -> 103 us (level)
  blocking collectives: 17.8 us -> 45.4 us
  starting transfers between devices: 39.9 us -> 24.7 us
  waiting for transfers between devices: 31.2 us -> 18.2 us
    all_to_all x1 -> x2, blocking collectives: 17.8 us -> 45.4 us  [exchange(): lax.all_to_all(packed, 'energy', split_axis=0, concat_axis=0, tiled=True)]
    all_to_all x2 -> x1, starting transfers between devices: 26.5 us -> 11.1 us  [exchange(): lax.all_to_all(packed, 'energy', split_axis=0, concat_axis=0, tiled=True)]
    ppermute x14, waiting for transfers between devices: 22 us -> 13.5 us  [move(): return lax.ppermute(value, 'space', pairs)]
    all_to_all x2 -> x1, waiting for transfers between devices: 9.28 us -> 4.69 us  [exchange(): lax.all_to_all(packed, 'energy', split_axis=0, concat_axis=0, tiled=True)]
    unnamed x26 -> x22, local copies, waits for them, and re-layouts: 2.26 us -> 3.09 us
  transfers between devices with their start and end apart: 16 -> 15, of which waited for: 4 -> 2; matrix products, arithmetic and copies ran while one was open for 0% -> 0% of each run, Pallas kernels for 8% -> 6%
where the time goes in v3:
time: 103 us
  blocking collectives  45.4 us (44%)
  starting transfers between devices  24.7 us (24%)
  waiting for transfers between devices  18.2 us (18%)
  Pallas kernels  10.7 us (10%)
  local copies, waits for them, and re-layouts  3.09 us (3%)
    all_to_all x2, blocking collectives, exchange(): lax.all_to_all(packed, 'energy', split_axis=0, concat_axis=0, tiled=True)  45.4 us
    ppermute x14, starting transfers between devices, move(): return lax.ppermute(value, 'space', pairs)  13.6 us
    ppermute x14, waiting for transfers between devices, move(): return lax.ppermute(value, 'space', pairs)  13.5 us
    all_to_all x1, starting transfers between devices, exchange(): lax.all_to_all(packed, 'energy', split_axis=0, concat_axis=0, tiled=True)  11.1 us
    all_to_all x1, waiting for transfers between devices, exchange(): lax.all_to_all(packed, 'energy', split_axis=0, concat_axis=0, tiled=True)  4.69 us
    unnamed x22, local copies, waits for them, and re-layouts  3.09 us
    pallas_call x3, Pallas kernels, after(): pl.pallas_call(body, out_shape=out_shape, in_specs=specs, compiler_params...  2.26 us
  transfers between devices with their start and end apart: 15, of which 2 were waited for; matrix products, arithmetic and copies ran while one was open for 0% of the time, Pallas kernels for 6%

profile of v3, /device:TPU:897, one launch (start us, length us, event | category | flops | bytes accessed | tf_op | source)
XLA Modules:
  0.0 102.5 jit_solution(3329608720738036003)
XLA Ops:
  0.0 3.4 %collective-permute-start.8 = (f32[2,384,384]{2,1,0:T(8,128)}, f32[2,384,384]{2,1,0:T(8,128)}, u32[]{:S(2)}, u32[]{:S(2)}) collective-permute-start(f32[2,384,384]{2,1,0:T(8,128)} %map_ref.2), channel_id=1, source_target_pairs={{8,7},{11,10},{14,13},{24,23},{27,26},{30,29},{40,39},{43,42},{46,... | collective-permute-start | bytes 3538952 | tf_op jit(solution)/shard_map/ppermute | solution.py:345
  3.4 0.7 collective-permute-start.6
  4.1 0.7 collective-permute-start
  4.8 0.0 copy-start.4
  4.8 0.9 copy-done.4
  5.7 1.1 %shard_map.115 = f32[64,8,128]{2,1,0:T(8,128)} custom-call(f32[2,32,1024]{2,1,0:T(8,128)S(1)} %bitcast.16), custom_call_target="tpu_custom_call" | custom-call | tf_op jit(solution)/shard_map/pallas_call | solution.py:185
  6.8 11.1 %all-to-all-start = ((f32[64,8,128]{2,1,0:T(8,128)}), f32[64,8,128]{2,1,0:T(8,128)S(1)}, u32[]{:S(2)}, u32[]{:S(2)}) async-start(f32[64,8,128]{2,1,0:T(8,128)} %shard_map.115), calls=%async_computation | async-start | bytes 524288 | tf_op jit(solution)/shard_map/all_to_all | solution.py:336
  17.9 0.0 copy-start.2
  17.9 1.3 %copy-done.2 = f32[2,384,384]{2,1,0:T(8,128)S(1)} copy-done((f32[2,384,384]{2,1,0:T(8,128)S(1)}, f32[2,384,384]{2,1,0:T(8,128)}, u32[]{:S(2)}) %copy-start.2) | copy-done | bytes 1179672
  19.1 0.2 shard_map.109
  19.4 0.0 collective-permute-done.arrived_ref
  19.4 0.0 copy-done
  19.4 0.7 collective-permute-start.1
  20.1 0.0 collective-permute-done.1.arrived_ref
  20.2 0.7 collective-permute-start.2
  20.8 0.0 collective-permute-done.2.arrived_ref
  20.9 0.7 collective-permute-start.3
  21.6 0.0 collective-permute-done.3.arrived_ref
  21.6 0.0 copy-start.6
  21.6 0.0 copy-start.8
  21.6 0.0 copy-start.9
  21.6 0.0 copy-start.3
  21.7 0.8 collective-permute-start.4
  22.5 0.7 collective-permute-start.7
  23.1 1.3 %collective-permute-start.9 = (f32[64,384]{1,0:T(8,128)S(1)}, f32[64,384]{1,0:T(8,128)S(1)}, u32[]{:S(2)}, u32[]{:S(2)}) collective-permute-start(f32[64,384]{1,0:T(8,128)S(1)} %bitcast.11), channel_id=1, source_target_pairs={{8,7},{11,10},{14,13},{24,23},{27,26},{30,29},{40,39},{43,42},{46,... | collective-permute-start | bytes 294920 | tf_op jit(solution)/shard_map/ppermute | solution.py:345
  24.4 0.0 collective-permute-done.4.arrived_ref
  24.5 0.7 collective-permute-start.5
  25.2 4.7 %all-to-all-done.refs_4_.packed_ref = f32[64,8,128]{2,1,0:T(8,128)S(1)} async-done(((f32[64,8,128]{2,1,0:T(8,128)}), f32[64,8,128]{2,1,0:T(8,128)S(1)}, u32[]{:S(2)}, u32[]{:S(2)}) %all-to-all-start) | async-done | bytes 262176 | tf_op jit(solution)/shard_map/all_to_all | solution.py:336
  29.8 0.0 copy-done.6
  29.8 0.0 copy-done.8
  29.8 0.0 copy-done.9
  29.9 0.0 copy-start.7
  29.9 0.8 copy-done.7
  30.7 0.5 shard_map.116
  31.2 0.0 copy-done.3
  31.2 1.1 %shard_map.117.refs_1_.screened_ref = f32[2,512,128]{2,1,0:T(8,128)S(1)} custom-call(f32[64,8,128]{2,1,0:T(8,128)S(1)} %all-to-all-done.refs_4_.packed_ref, bf16[512,1024]{1,0:T(8,128)(2,1)S(1)} %get-tuple-element.47.high_ref, bf16[512,1024]{1,0:T(8,128)(2,1)S(1)} %get-tuple-element.48.low_ref, f32[2,512,128]{2,1,0:T(8,128)S(1)} %get-tuple-element.49.twiddle_ref, ...), custom_call_target="tpu_custom_call" | custom-call | tf_op jit(solution)/shard_map/pallas_call | solution.py:327
  32.4 0.0 collective-permute-done.8.refs_0_
  32.4 1.5 %shard_map.119 = (bf16[384,768]{1,0:T(8,128)(2,1)S(1)}, bf16[384,768]{1,0:T(8,128)(2,1)S(1)}) custom-call(f32[2,384,384]{2,1,0:T(8,128)} %collective-permute-done.8.refs_0_, f32[2,512,128]{2,1,0:T(8,128)S(1)} %shard_map.117.refs_1_.screened_ref), custom_call_target="tpu_custom_call" | custom-call | tf_op jit(solution)/shard_map/pallas_call | solution.py:30
  33.9 0.0 collective-permute-done.6.refs_0_
  33.9 0.2 shard_map.118
  34.1 0.0 collective-permute-done.7.refs_2_
  34.1 0.0 collective-permute-done.9.refs_8_
  34.1 0.0 collective-permute-done.5.arrived_ref
  34.2 0.7 collective-permute-start.10
  34.9 0.0 collective-permute-done.10.arrived_ref
  34.9 0.7 collective-permute-start.11
  35.6 0.0 collective-permute-done.11.arrived_ref
  35.6 0.0 copy-start.1
  35.7 0.8 collective-permute-start.12
  36.5 0.0 copy-start.10
  36.5 1.3 %collective-permute-start.13 = (f32[64,384]{1,0:T(8,128)S(1)}, f32[64,384]{1,0:T(8,128)S(1)}, u32[]{:S(2)}, u32[]{:S(2)}) collective-permute-start(f32[64,384]{1,0:T(8,128)S(1)} %get-tuple-element.63), channel_id=1, source_target_pairs={{7,8},{10,11},{13,14},{23,24},{26,27},{29,30},{39,40},{42,43},{45,... | collective-permute-start | bytes 294920 | tf_op jit(solution)/shard_map/ppermute | solution.py:345
  37.8 0.0 copy-done.1
  37.8 0.3 shard_map.123
  38.1 0.0 copy-done.10
  38.1 0.0 copy-start.5
  38.2 1.0 shard_map.124.chosen_ref
  39.1 0.0 collective-permute-done.12.arrived_ref
  39.1 13.5 %collective-permute-done.13.other_ref = f32[64,384]{1,0:T(8,128)S(1)} collective-permute-done((f32[64,384]{1,0:T(8,128)S(1)}, f32[64,384]{1,0:T(8,128)S(1)}, u32[]{:S(2)}, u32[]{:S(2)}) %collective-permute-start.13) | collective-permute-done | bytes 98336 | tf_op jit(solution)/shard_map/ppermute | solution.py:345
  52.6 0.0 copy-done.5
  52.6 1.4 %shard_map.125 = f32[64,8,128]{2,1,0:T(8,128)S(1)} custom-call(f32[64,384]{1,0:T(8,128)S(1)} %collective-permute-done.12.arrived_ref, f32[64,384]{1,0:T(8,128)S(1)} %collective-permute-done.13.other_ref, f32[64,384]{1,0:T(8,128)S(1)} %get-tuple-element.64.entering_ref, bf16[384,1536]{1,0:T(8,128)(2,1)S(1)} %get-tuple-element.65.high_ref, ...), custom_call_target="tpu_custom_call" | custom-call | tf_op jit(solution)/shard_map/pallas_call | solution.py:232
  54.1 27.6 %all_to_all.15.packed_ref = f32[64,8,128]{2,1,0:T(8,128)S(1)} all-to-all(f32[64,8,128]{2,1,0:T(8,128)S(1)} %shard_map.125), channel_id=1, replica_groups=mesh['energy'=64,'space'=16] {'energy'}, dimensions={0} | all-to-all | bytes 524288 | tf_op jit(solution)/shard_map/all_to_all | solution.py:336
  81.6 2.0 %shard_map.126 = f32[64,8,128]{2,1,0:T(8,128)S(1)} custom-call(f32[64,8,128]{2,1,0:T(8,128)S(1)} %all_to_all.15.packed_ref, f32[2,512,128]{2,1,0:T(8,128)S(1)} %shard_map.117.refs_1_.screened_ref, bf16[512,1024]{1,0:T(8,128)(2,1)S(1)} %get-tuple-element.47.high_ref, bf16[512,1024]{1,0:T(8,128)(2,1)S(1)} %get-tuple-element.48.low_ref, ...), custom_call_target="tpu_custom_call" | custom-call | tf_op jit(solution)/shard_map/pallas_call | solution.py:332
  83.6 17.8 %all_to_all.16.packed_ref = f32[64,8,128]{2,1,0:T(8,128)S(1)} all-to-all(f32[64,8,128]{2,1,0:T(8,128)S(1)} %shard_map.126), channel_id=1, replica_groups=mesh['energy'=64,'space'=16] {'energy'}, dimensions={0} | all-to-all | bytes 524288 | tf_op jit(solution)/shard_map/all_to_all | solution.py:336
  101.4 1.1 %shard_map.127 = f32[2,32,1024]{2,1,0:T(8,128)} custom-call(f32[64,8,128]{2,1,0:T(8,128)S(1)} %all_to_all.16.packed_ref), custom_call_target="tpu_custom_call" | custom-call | tf_op jit(solution)/shard_map/pallas_call | solution.py:190
  (9 shorter events, 0.3 us)
Async XLA Ops:
  0.0 19.4 %copy-start = (f32[2,32,384]{2,1,0:T(8,128)S(1)}, f32[2,32,384]{2,1,0:T(8,128)}, u32[]{:S(2)}) copy-start(f32[2,32,384]{2,1,0:T(8,128)} %param.12) | copy-start | bytes 294916
  0.0 32.4 %collective-permute-start.8 = (f32[2,384,384]{2,1,0:T(8,128)}, f32[2,384,384]{2,1,0:T(8,128)}, u32[]{:S(2)}, u32[]{:S(2)}) collective-permute-start(f32[2,384,384]{2,1,0:T(8,128)} %map_ref.2), channel_id=1, source_target_pairs={{8,7},{11,10},{14,13},{24,23},{27,26},{30,29},{40,39},{43,42},{46,... | collective-permute-start | bytes 3538952 | tf_op jit(solution)/shard_map/ppermute | solution.py:345
  3.4 30.5 %collective-permute-start.6 = (f32[2,384,384]{2,1,0:T(8,128)}, f32[2,384,384]{2,1,0:T(8,128)S(1)}, u32[]{:S(2)}, u32[]{:S(2)}) collective-permute-start(f32[2,384,384]{2,1,0:T(8,128)} %map_ref.2), channel_id=1, source_target_pairs={{6,7},{9,10},{12,13},{22,23},{25,26},{28,29},{38,39},{41,42},{44,4... | collective-permute-start | bytes 3538952 | tf_op jit(solution)/shard_map/ppermute | solution.py:345
  4.1 15.3 %collective-permute-start = (f32[64,384]{1,0:T(8,128)}, f32[64,384]{1,0:T(8,128)S(1)}, u32[]{:S(2)}, u32[]{:S(2)}) collective-permute-start(f32[64,384]{1,0:T(8,128)} %bitcast.5), channel_id=1, source_target_pairs={{0,1},{16,17},{32,33},{48,49},{64,65},{80,81},{96,97},{112,113},{1... | collective-permute-start | bytes 294920 | tf_op jit(solution)/shard_map/ppermute | solution.py:345
  4.8 1.0 copy-start.4
  6.8 23.0 %all-to-all-start = ((f32[64,8,128]{2,1,0:T(8,128)}), f32[64,8,128]{2,1,0:T(8,128)S(1)}, u32[]{:S(2)}, u32[]{:S(2)}) async-start(f32[64,8,128]{2,1,0:T(8,128)} %shard_map.115), calls=%async_computation | async-start | bytes 524288 | tf_op jit(solution)/shard_map/all_to_all | solution.py:336
  17.9 1.3 %copy-start.2 = (f32[2,384,384]{2,1,0:T(8,128)S(1)}, f32[2,384,384]{2,1,0:T(8,128)}, u32[]{:S(2)}) copy-start(f32[2,384,384]{2,1,0:T(8,128)} %map_ref.2) | copy-start | bytes 3538948
  19.4 0.7 collective-permute-start.1
  20.2 0.7 collective-permute-start.2
  20.9 0.7 collective-permute-start.3
  21.6 8.2 %copy-start.6 = (f32[2,32,512]{2,1,0:T(8,128)S(1)}, f32[2,32,512]{2,1,0:T(8,128)}, u32[]{:S(2)}) copy-start(f32[2,32,512]{2,1,0:T(8,128)} %constant.15.clone.refs_1_) | copy-start | bytes 393220
  21.6 8.2 %copy-start.8 = (f32[2,32,128]{2,1,0:T(8,128)S(1)}, f32[2,32,128]{2,1,0:T(8,128)}, u32[]{:S(2)}) copy-start(f32[2,32,128]{2,1,0:T(8,128)} %constant.17.clone.refs_3_) | copy-start | bytes 98308
  21.6 8.2 %copy-start.9 = (f32[2,16,128]{2,1,0:T(8,128)S(1)}, f32[2,16,128]{2,1,0:T(8,128)}, u32[]{:S(2)}) copy-start(f32[2,16,128]{2,1,0:T(8,128)} %constant.16.clone.refs_2_) | copy-start | bytes 49156
  21.6 9.6 %copy-start.3 = (bf16[2,128,128]{2,1,0:T(8,128)(2,1)S(1)}, bf16[2,128,128]{2,1,0:T(8,128)(2,1)}, u32[]{:S(2)}) copy-start(bf16[2,128,128]{2,1,0:T(8,128)(2,1)} %constant.18.clone.lanes_ref) | copy-start | bytes 196612
  21.7 2.8 %collective-permute-start.4 = (f32[64,384]{1,0:T(8,128)S(1)}, f32[64,384]{1,0:T(8,128)S(1)}, u32[]{:S(2)}, u32[]{:S(2)}) collective-permute-start(f32[64,384]{1,0:T(8,128)S(1)} %get-tuple-element.44.refs_4_), channel_id=1, source_target_pairs={{4,5},{20,21},{36,37},{52,53},{68,69},{84,85},{100,101},{116,117},... | collective-permute-start | bytes 294920 | tf_op jit(solution)/shard_map/ppermute | solution.py:345
  22.5 11.7 %collective-permute-start.7 = (f32[64,384]{1,0:T(8,128)S(1)}, f32[64,384]{1,0:T(8,128)S(1)}, u32[]{:S(2)}, u32[]{:S(2)}) collective-permute-start(f32[64,384]{1,0:T(8,128)S(1)} %bitcast.10), channel_id=1, source_target_pairs={{6,7},{9,10},{12,13},{22,23},{25,26},{28,29},{38,39},{41,42},{44,4... | collective-permute-start | bytes 294920 | tf_op jit(solution)/shard_map/ppermute | solution.py:345
  23.1 11.0 %collective-permute-start.9 = (f32[64,384]{1,0:T(8,128)S(1)}, f32[64,384]{1,0:T(8,128)S(1)}, u32[]{:S(2)}, u32[]{:S(2)}) collective-permute-start(f32[64,384]{1,0:T(8,128)S(1)} %bitcast.11), channel_id=1, source_target_pairs={{8,7},{11,10},{14,13},{24,23},{27,26},{30,29},{40,39},{43,42},{46,... | collective-permute-start | bytes 294920 | tf_op jit(solution)/shard_map/ppermute | solution.py:345
  24.5 9.7 %collective-permute-start.5 = (f32[64,384]{1,0:T(8,128)S(1)}, f32[64,384]{1,0:T(8,128)S(1)}, u32[]{:S(2)}, u32[]{:S(2)}) collective-permute-start(f32[64,384]{1,0:T(8,128)S(1)} %get-tuple-element.46.refs_11_), channel_id=1, source_target_pairs={{5,7},{21,23},{37,39},{53,55},{69,71},{85,87},{101,103},{117,119},... | collective-permute-start | bytes 294920 | tf_op jit(solution)/shard_map/ppermute | solution.py:345
  29.9 0.8 copy-start.7
  34.2 0.7 collective-permute-start.10
  34.9 0.7 collective-permute-start.11
  35.6 2.2 %copy-start.1 = (f32[2,384,768]{2,1,0:T(8,128)S(1)}, f32[2,384,768]{2,1,0:T(8,128)}, u32[]{:S(2)}) copy-start(f32[2,384,768]{2,1,0:T(8,128)} %map_ref.3) | copy-start | bytes 7077892
  35.7 3.4 %collective-permute-start.12 = (f32[64,384]{1,0:T(8,128)S(1)}, f32[64,384]{1,0:T(8,128)S(1)}, u32[]{:S(2)}, u32[]{:S(2)}) collective-permute-start(f32[64,384]{1,0:T(8,128)S(1)} %get-tuple-element.62), channel_id=1, source_target_pairs={{5,6},{7,9},{10,12},{13,15},{21,22},{23,25},{26,28},{29,31},{37,38... | collective-permute-start | bytes 294920 | tf_op jit(solution)/shard_map/ppermute | solution.py:345
  36.5 1.7 %copy-start.10 = (s32[2,1024]{1,0:T(2,128)S(1)}, s32[2,1024]{1,0:T(2,128)}, u32[]{:S(2)}) copy-start(s32[2,1024]{1,0:T(2,128)} %pairs_ref.1) | copy-start | bytes 24580
  36.5 16.1 %collective-permute-start.13 = (f32[64,384]{1,0:T(8,128)S(1)}, f32[64,384]{1,0:T(8,128)S(1)}, u32[]{:S(2)}, u32[]{:S(2)}) collective-permute-start(f32[64,384]{1,0:T(8,128)S(1)} %get-tuple-element.63), channel_id=1, source_target_pairs={{7,8},{10,11},{13,14},{23,24},{26,27},{29,30},{39,40},{42,43},{45,... | collective-permute-start | bytes 294920 | tf_op jit(solution)/shard_map/ppermute | solution.py:345
  38.1 14.5 %copy-start.5 = (f32[2,768,32]{1,2,0:T(8,128)S(1)}, f32[2,768,32]{1,2,0:T(8,128)}, u32[]{:S(2)}) copy-start(f32[2,768,32]{1,2,0:T(8,128)} %param.14) | copy-start | bytes 589828

commit v4 on v3

--- a/solution.py
+++ b/solution.py
@@ -21,8 +21,8 @@
         vmem = pl.BlockSpec(memory_space=pltpu.VMEM)
 
         def after(*operands):
-            specs = [vmem] * (len(operands) - 1) + [pl.BlockSpec(memory_space=pl.ANY)]
             count = len(operands) - 1
+            specs = [vmem] * count + [pl.BlockSpec(memory_space=pl.ANY)]
 
             def body(*refs):
                 kernel(*refs[:count], *refs[count + 1 :])
@@ -31,6 +31,7 @@
                 body,
                 out_shape=out_shape,
                 in_specs=specs,
+                scratch_shapes=list(scratch),
                 compiler_params=pltpu.CompilerParams(vmem_limit_bytes=megabytes << 20),
             )(*operands)
 
@@ -180,9 +181,10 @@
             values_ref[part, :, group * 128 : (group + 1) * 128] = stage_ref[part, group]
 
 
-def pack_array(values):
+def pack_array(values, awaited):
     shape = jax.ShapeDtypeStruct((64, 8, 128), f32)
-    return call(pack_kernel, shape, 4, [pltpu.VMEM((2, 8, 32, 128), f32)])(values)
+    scratch = [pltpu.VMEM((2, 8, 32, 128), f32)]
+    return call(pack_kernel, shape, 4, scratch, True)(values, awaited)
 
 
 def unpack_array(packed):
@@ -347,27 +349,34 @@
     arrived = move(source, (0, 1))
     upward = [(leader - 1, leader) for leader in LEADERS]
     downward = [(leader + 1, leader) for leader in LEADERS]
-    before = (move(chain_map, *upward), move(source, *upward))
-    after = (move(chain_map, *downward), move(source, *downward))
+    maps = []
+    for order, chosen in enumerate((slice(0, 1), slice(1, None))):
+        maps.append([move(chain_map, *pairs[chosen]) for pairs in (upward, downward)])
+        if order == 0:
+            source_before, source_after = move(source, *upward), move(source, *downward)
     own = (*split_map(chain_map), source)
     entering, middle, state = on_plane(first_kernel, 1, place, (arrived, *own), (), (source,) * 3)
     for number in range(2, SINGLES + 1):
         arrived = move(state, (number - 1, number))
+        if number == SINGLES - 1:
+            screened = pack_array(jnp.swapaxes(interaction, 1, 2), entering)
+            screened = exchange(screened)
         entering, state = on_plane(
             single_kernel, number, place, (arrived, *own), (entering, state)
         )
-    screened = exchange(pack_array(jnp.swapaxes(interaction, 1, 2)))
-    constants = tables(screened)
-    screened = screened_spectrum(screened, constants)
-    before = (*split_map(before[0], screened), before[1])
-    after = (*split_map(after[0], screened), after[1])
-    last = SINGLES
-    for leader in LEADERS:
+    last, awaited = SINGLES, ()
+    for order, leader in enumerate(LEADERS):
         arrived = move(state, (last, leader))
-        operands = (arrived, *before, *own, *after)
+        if order < 2:
+            before, after = (split_map(value, *awaited) for value in maps[order])
+        operands = (arrived, *before, source_before, *own, *after, source_after)
         entering, middle, state = on_plane(
             triple_kernel, leader, place, operands, (entering, middle, state)
         )
+        if order == 0:
+            constants = tables(entering)
+            screened = screened_spectrum(screened, constants)
+            awaited = (screened,)
         last = leader
     arrived = move(state, (SINGLES, SINGLES + 1), *((leader, leader + 2) for leader in LEADERS))
     other = move(middle, *((leader, leader + 1) for leader in LEADERS))

time: 103 us -> 116 us (1.13)
  Pallas kernels: 10.7 us -> 16.3 us
  starting transfers between devices: 24.7 us -> 28.9 us
  local copies, waits for them, and re-layouts: 3.09 us -> 4.54 us
    ppermute x14 -> x16, waiting for transfers between devices: 13.5 us -> 19.1 us  [move(): return lax.ppermute(value, 'space', pairs)]
    all_to_all x1, waiting for transfers between devices: 4.69 us -> 0.01 us  [exchange(): lax.all_to_all(packed, 'energy', split_axis=0, concat_axis=0, tiled=True)]
    ppermute x14 -> x16, starting transfers between devices: 13.6 us -> 17.6 us  [move(): return lax.ppermute(value, 'space', pairs)]
    pallas_call x2 -> x4, Pallas kernels: 0.54 us -> 2.27 us  [split_map(): call(split_kernel, [shape, shape], 8, (), bool(awaited))(value, *awaited)]
    pallas_call x8, Pallas kernels: 0.26 us -> 1.83 us  [on_plane(): pl.pallas_call(functools.partial(kernel, number), out_shape=[jax.ShapeDty...]
    unnamed x22 -> x40, local copies, waits for them, and re-layouts: 3.09 us -> 4.54 us
    pallas_call x4, Pallas kernels: 3.34 us -> 4.67 us  [after(): pl.pallas_call(body, out_shape=out_shape, in_specs=specs, scratch_shapes=...]
  transfers between devices with their start and end apart: 15 -> 17, of which waited for: 2 -> 2; matrix products, arithmetic and copies ran while one was open for 0% -> 0% of each run, Pallas kernels for 6% -> 9%
where the time goes in v4:
time: 116 us; the launch traced here: 115 us
  blocking collectives  46.2 us (40%)
  starting transfers between devices  28.9 us (25%)
  waiting for transfers between devices  19.1 us (16%)
  Pallas kernels  16.3 us (14%)
  local copies, waits for them, and re-layouts  4.54 us (4%)
    all_to_all x2, blocking collectives, exchange(): lax.all_to_all(packed, 'energy', split_axis=0, concat_axis=0, tiled=True)  46.2 us
    ppermute x16, waiting for transfers between devices, move(): return lax.ppermute(value, 'space', pairs)  19.1 us
    ppermute x16, starting transfers between devices, move(): return lax.ppermute(value, 'space', pairs)  17.6 us
    all_to_all x1, starting transfers between devices, exchange(): lax.all_to_all(packed, 'energy', split_axis=0, concat_axis=0, tiled=True)  11.3 us
    pallas_call x4, Pallas kernels, after(): pl.pallas_call(body, out_shape=out_shape, in_specs=specs, scratch_shapes=...  4.67 us
    unnamed x40, local copies, waits for them, and re-layouts  4.54 us
  transfers between devices with their start and end apart: 17, of which 2 were waited for; matrix products, arithmetic and copies ran while one was open for 0% of the time, Pallas kernels for 9%

profile of v4, /device:TPU:897, one launch (start us, length us, event | category | flops | bytes accessed | tf_op | source)
XLA Modules:
  0.0 115.5 jit_solution(10077444731632927680)
XLA Ops:
  0.0 0.9 collective-permute-start.6
  0.9 1.7 %collective-permute-start.8 = (f32[2,384,384]{2,1,0:T(8,128)}, f32[2,384,384]{2,1,0:T(8,128)}, u32[]{:S(2)}, u32[]{:S(2)}) collective-permute-start(f32[2,384,384]{2,1,0:T(8,128)} %map_ref.2), channel_id=1, source_target_pairs={{8,7},{24,23},{40,39},{56,55},{72,71},{88,87},{104,103},{120,119},... | collective-permute-start | bytes 3538952 | tf_op jit(solution)/shard_map/ppermute | solution.py:347
  2.6 3.2 %collective-permute-start.12 = (f32[2,384,384]{2,1,0:T(8,128)}, f32[2,384,384]{2,1,0:T(8,128)}, u32[]{:S(2)}, u32[]{:S(2)}) collective-permute-start(f32[2,384,384]{2,1,0:T(8,128)} %map_ref.2), channel_id=1, source_target_pairs={{11,10},{14,13},{27,26},{30,29},{43,42},{46,45},{59,58},{62,61},{7... | collective-permute-start | bytes 3538952 | tf_op jit(solution)/shard_map/ppermute | solution.py:347
  5.8 1.7 %collective-permute-start.11 = (f32[2,384,384]{2,1,0:T(8,128)}, f32[2,384,384]{2,1,0:T(8,128)}, u32[]{:S(2)}, u32[]{:S(2)}) collective-permute-start(f32[2,384,384]{2,1,0:T(8,128)} %map_ref.2), channel_id=1, source_target_pairs={{9,10},{12,13},{25,26},{28,29},{41,42},{44,45},{57,58},{60,61},{73... | collective-permute-start | bytes 3538952 | tf_op jit(solution)/shard_map/ppermute | solution.py:347
  7.5 0.7 collective-permute-start
  8.2 1.3 %copy-done.5 = f32[2,384,384]{2,1,0:T(8,128)S(1)} copy-done((f32[2,384,384]{2,1,0:T(8,128)S(1)}, f32[2,384,384]{2,1,0:T(8,128)}, u32[]{:S(2)}) %copy-start.5) | copy-done | bytes 1179672
  9.4 0.2 shard_map.109
  9.7 0.0 collective-permute-done.arrived_ref
  9.7 0.7 collective-permute-start.1
  10.4 0.0 collective-permute-done.1.arrived_ref
  10.4 0.0 copy-start.11
  10.5 0.8 collective-permute-start.2
  11.3 0.0 collective-permute-done.2.arrived_ref
  11.3 0.1 copy-done.11
  11.4 1.1 shard_map.118
  12.5 11.3 %all-to-all-start = ((f32[64,8,128]{2,1,0:T(8,128)}), f32[64,8,128]{2,1,0:T(8,128)}, u32[]{:S(2)}, u32[]{:S(2)}) async-start(f32[64,8,128]{2,1,0:T(8,128)} %shard_map.118), calls=%async_computation | async-start | bytes 524288 | tf_op jit(solution)/shard_map/all_to_all | solution.py:338
  23.7 0.7 collective-permute-start.3
  24.4 0.0 collective-permute-done.3.arrived_ref
  24.5 0.7 collective-permute-start.4
  25.1 0.0 collective-permute-done.4.arrived_ref
  25.2 0.7 collective-permute-start.7
  25.9 0.0 collective-permute-done.6.map_ref
  25.9 1.3 %collective-permute-start.9 = (f32[64,384]{1,0:T(8,128)S(1)}, f32[64,384]{1,0:T(8,128)S(1)}, u32[]{:S(2)}, u32[]{:S(2)}) collective-permute-start(f32[64,384]{1,0:T(8,128)S(1)} %bitcast.12), channel_id=1, source_target_pairs={{8,7},{11,10},{14,13},{24,23},{27,26},{30,29},{40,39},{43,42},{46,... | collective-permute-start | bytes 294920 | tf_op jit(solution)/shard_map/ppermute | solution.py:347
  27.2 0.0 collective-permute-done.8.map_ref
  27.2 0.7 collective-permute-start.5
  27.9 0.2 shard_map.115
  28.1 1.5 %shard_map.116 = (bf16[384,768]{1,0:T(8,128)(2,1)S(1)}, bf16[384,768]{1,0:T(8,128)(2,1)S(1)}) custom-call(f32[2,384,384]{2,1,0:T(8,128)} %collective-permute-done.8.map_ref), custom_call_target="tpu_custom_call" | custom-call | tf_op jit(solution)/shard_map/pallas_call | solution.py:77
  29.6 0.0 collective-permute-done.7.refs_2_
  29.6 2.1 %collective-permute-done.9.refs_8_ = f32[64,384]{1,0:T(8,128)S(1)} collective-permute-done((f32[64,384]{1,0:T(8,128)S(1)}, f32[64,384]{1,0:T(8,128)S(1)}, u32[]{:S(2)}, u32[]{:S(2)}) %collective-permute-start.9) | collective-permute-done | bytes 98336 | tf_op jit(solution)/shard_map/ppermute | solution.py:347
  31.7 0.0 collective-permute-done.5.arrived_ref
  31.7 0.0 copy-start.17
  31.7 0.0 copy-start.18
  31.7 0.0 copy-start.10
  31.7 0.7 shard_map.117
  32.4 0.6 copy-done.14
  33.1 1.3 %collective-permute-start.10 = (f32[64,384]{1,0:T(8,128)}, f32[64,384]{1,0:T(8,128)}, u32[]{:S(2)}, u32[]{:S(2)}) collective-permute-start(f32[64,384]{1,0:T(8,128)} %get-tuple-element.57.refs_11_), channel_id=1, source_target_pairs={{7,10},{23,26},{39,42},{55,58},{71,74},{87,90},{103,106},{119,122}... | collective-permute-start | bytes 294920 | tf_op jit(solution)/shard_map/ppermute | solution.py:347
  34.4 0.5 shard_map.119
  34.9 0.8 copy-done.2
  35.7 0.6 copy-done.8
  36.4 0.0 all-to-all-done.packed_ref
  36.4 1.0 copy-done.3
  37.4 2.1 %shard_map.120.refs_1_.screened_ref = f32[2,512,128]{2,1,0:T(8,128)S(1)} custom-call(f32[64,8,128]{2,1,0:T(8,128)} %all-to-all-done.packed_ref, bf16[512,1024]{1,0:T(8,128)(2,1)S(1)} %get-tuple-element.59.high_ref, bf16[512,1024]{1,0:T(8,128)(2,1)S(1)} %get-tuple-element.60.low_ref, f32[2,512,128]{2,1,0:T(8,128)S(1)} %copy-done.3, ...), custom_call_target="tpu_custom_call" | custom-call | tf_op jit(solution)/shard_map/pallas_call | solution.py:329
  39.5 0.0 collective-permute-done.12.refs_0_
  39.5 1.5 %shard_map.122 = (bf16[384,768]{1,0:T(8,128)(2,1)S(1)}, bf16[384,768]{1,0:T(8,128)(2,1)S(1)}) custom-call(f32[2,384,384]{2,1,0:T(8,128)} %collective-permute-done.12.refs_0_, f32[2,512,128]{2,1,0:T(8,128)S(1)} %shard_map.120.refs_1_.screened_ref), custom_call_target="tpu_custom_call" | custom-call | tf_op jit(solution)/shard_map/pallas_call | solution.py:30
  41.0 0.0 collective-permute-done.11.refs_0_
  41.0 1.6 %shard_map.121 = (bf16[384,768]{1,0:T(8,128)(2,1)S(1)}, bf16[384,768]{1,0:T(8,128)(2,1)S(1)}) custom-call(f32[2,384,384]{2,1,0:T(8,128)} %collective-permute-done.11.refs_0_, f32[2,512,128]{2,1,0:T(8,128)S(1)} %shard_map.120.refs_1_.screened_ref), custom_call_target="tpu_custom_call" | custom-call | tf_op jit(solution)/shard_map/pallas_call | solution.py:30
  42.6 0.0 collective-permute-done.10.arrived_ref
  42.6 1.0 shard_map.123
  43.6 0.7 collective-permute-start.13
  44.3 0.0 collective-permute-done.13.arrived_ref
  44.3 0.0 copy-start.1
  44.4 0.8 collective-permute-start.14
  45.2 0.0 copy-start.19
  45.2 1.3 %collective-permute-start.15 = (f32[64,384]{1,0:T(8,128)S(1)}, f32[64,384]{1,0:T(8,128)S(1)}, u32[]{:S(2)}, u32[]{:S(2)}) collective-permute-start(f32[64,384]{1,0:T(8,128)S(1)} %get-tuple-element.71), channel_id=1, source_target_pairs={{7,8},{10,11},{13,14},{23,24},{26,27},{29,30},{39,40},{42,43},{45,... | collective-permute-start | bytes 294920 | tf_op jit(solution)/shard_map/ppermute | solution.py:347
  46.5 0.3 shard_map.125
  46.8 0.0 copy-start.12
  46.8 1.0 shard_map.126.chosen_ref
  47.8 0.0 collective-permute-done.14.arrived_ref
  47.8 16.9 %collective-permute-done.15.other_ref = f32[64,384]{1,0:T(8,128)S(1)} collective-permute-done((f32[64,384]{1,0:T(8,128)S(1)}, f32[64,384]{1,0:T(8,128)S(1)}, u32[]{:S(2)}, u32[]{:S(2)}) %collective-permute-start.15) | collective-permute-done | bytes 98336 | tf_op jit(solution)/shard_map/ppermute | solution.py:347
  64.8 1.4 %shard_map.127 = f32[64,8,128]{2,1,0:T(8,128)S(1)} custom-call(f32[64,384]{1,0:T(8,128)S(1)} %collective-permute-done.14.arrived_ref, f32[64,384]{1,0:T(8,128)S(1)} %collective-permute-done.15.other_ref, f32[64,384]{1,0:T(8,128)S(1)} %get-tuple-element.72.entering_ref, bf16[384,1536]{1,0:T(8,128)(2,1)S(1)} %get-tuple-element.73.high_ref, ...), custom_call_target="tpu_custom_call" | custom-call | tf_op jit(solution)/shard_map/pallas_call | solution.py:234
  66.2 28.4 %all_to_all.15.packed_ref = f32[64,8,128]{2,1,0:T(8,128)S(1)} all-to-all(f32[64,8,128]{2,1,0:T(8,128)S(1)} %shard_map.127), channel_id=1, replica_groups=mesh['energy'=64,'space'=16] {'energy'}, dimensions={0} | all-to-all | bytes 524288 | tf_op jit(solution)/shard_map/all_to_all | solution.py:338
  94.6 2.0 %shard_map.128 = f32[64,8,128]{2,1,0:T(8,128)S(1)} custom-call(f32[64,8,128]{2,1,0:T(8,128)S(1)} %all_to_all.15.packed_ref, f32[2,512,128]{2,1,0:T(8,128)S(1)} %shard_map.120.refs_1_.screened_ref, bf16[512,1024]{1,0:T(8,128)(2,1)S(1)} %get-tuple-element.59.high_ref, bf16[512,1024]{1,0:T(8,128)(2,1)S(1)} %get-tuple-element.60.low_ref, ...), custom_call_target="tpu_custom_call" | custom-call | tf_op jit(solution)/shard_map/pallas_call | solution.py:334
  96.6 17.8 %all_to_all.16.packed_ref = f32[64,8,128]{2,1,0:T(8,128)S(1)} all-to-all(f32[64,8,128]{2,1,0:T(8,128)S(1)} %shard_map.128), channel_id=1, replica_groups=mesh['energy'=64,'space'=16] {'energy'}, dimensions={0} | all-to-all | bytes 524288 | tf_op jit(solution)/shard_map/all_to_all | solution.py:338
  114.4 1.1 shard_map.129
  (33 shorter events, 0.2 us)
Async XLA Ops:
  0.0 9.7 %copy-start = (f32[2,32,384]{2,1,0:T(8,128)S(1)}, f32[2,32,384]{2,1,0:T(8,128)}, u32[]{:S(2)}) copy-start(f32[2,32,384]{2,1,0:T(8,128)} %param.12) | copy-start | bytes 294916
  0.0 25.9 %collective-permute-start.6 = (f32[2,384,384]{2,1,0:T(8,128)}, f32[2,384,384]{2,1,0:T(8,128)S(1)}, u32[]{:S(2)}, u32[]{:S(2)}) collective-permute-start(f32[2,384,384]{2,1,0:T(8,128)} %map_ref.2), channel_id=1, source_target_pairs={{6,7},{22,23},{38,39},{54,55},{70,71},{86,87},{102,103},{118,119},... | collective-permute-start | bytes 3538952 | tf_op jit(solution)/shard_map/ppermute | solution.py:347
  0.9 26.3 %collective-permute-start.8 = (f32[2,384,384]{2,1,0:T(8,128)}, f32[2,384,384]{2,1,0:T(8,128)}, u32[]{:S(2)}, u32[]{:S(2)}) collective-permute-start(f32[2,384,384]{2,1,0:T(8,128)} %map_ref.2), channel_id=1, source_target_pairs={{8,7},{24,23},{40,39},{56,55},{72,71},{88,87},{104,103},{120,119},... | collective-permute-start | bytes 3538952 | tf_op jit(solution)/shard_map/ppermute | solution.py:347
  2.6 36.9 %collective-permute-start.12 = (f32[2,384,384]{2,1,0:T(8,128)}, f32[2,384,384]{2,1,0:T(8,128)}, u32[]{:S(2)}, u32[]{:S(2)}) collective-permute-start(f32[2,384,384]{2,1,0:T(8,128)} %map_ref.2), channel_id=1, source_target_pairs={{11,10},{14,13},{27,26},{30,29},{43,42},{46,45},{59,58},{62,61},{7... | collective-permute-start | bytes 3538952 | tf_op jit(solution)/shard_map/ppermute | solution.py:347
  5.8 35.2 %collective-permute-start.11 = (f32[2,384,384]{2,1,0:T(8,128)}, f32[2,384,384]{2,1,0:T(8,128)}, u32[]{:S(2)}, u32[]{:S(2)}) collective-permute-start(f32[2,384,384]{2,1,0:T(8,128)} %map_ref.2), channel_id=1, source_target_pairs={{9,10},{12,13},{25,26},{28,29},{41,42},{44,45},{57,58},{60,61},{73... | collective-permute-start | bytes 3538952 | tf_op jit(solution)/shard_map/ppermute | solution.py:347
  7.5 2.2 %collective-permute-start = (f32[64,384]{1,0:T(8,128)}, f32[64,384]{1,0:T(8,128)S(1)}, u32[]{:S(2)}, u32[]{:S(2)}) collective-permute-start(f32[64,384]{1,0:T(8,128)} %bitcast.5), channel_id=1, source_target_pairs={{0,1},{16,17},{32,33},{48,49},{64,65},{80,81},{96,97},{112,113},{1... | collective-permute-start | bytes 294920 | tf_op jit(solution)/shard_map/ppermute | solution.py:347
  8.2 1.3 %copy-start.5 = (f32[2,384,384]{2,1,0:T(8,128)S(1)}, f32[2,384,384]{2,1,0:T(8,128)}, u32[]{:S(2)}) copy-start(f32[2,384,384]{2,1,0:T(8,128)} %map_ref.2) | copy-start | bytes 3538948
  9.7 0.7 collective-permute-start.1
  10.4 1.0 copy-start.11
  10.5 0.8 collective-permute-start.2
  12.5 23.9 %all-to-all-start = ((f32[64,8,128]{2,1,0:T(8,128)}), f32[64,8,128]{2,1,0:T(8,128)}, u32[]{:S(2)}, u32[]{:S(2)}) async-start(f32[64,8,128]{2,1,0:T(8,128)} %shard_map.118), calls=%async_computation | async-start | bytes 524288 | tf_op jit(solution)/shard_map/all_to_all | solution.py:338
  23.7 0.7 collective-permute-start.3
  24.5 0.7 collective-permute-start.4
  25.2 4.4 %collective-permute-start.7 = (f32[64,384]{1,0:T(8,128)S(1)}, f32[64,384]{1,0:T(8,128)S(1)}, u32[]{:S(2)}, u32[]{:S(2)}) collective-permute-start(f32[64,384]{1,0:T(8,128)S(1)} %bitcast.10), channel_id=1, source_target_pairs={{6,7},{9,10},{12,13},{22,23},{25,26},{28,29},{38,39},{41,42},{44,4... | collective-permute-start | bytes 294920 | tf_op jit(solution)/shard_map/ppermute | solution.py:347
  25.9 5.8 %collective-permute-start.9 = (f32[64,384]{1,0:T(8,128)S(1)}, f32[64,384]{1,0:T(8,128)S(1)}, u32[]{:S(2)}, u32[]{:S(2)}) collective-permute-start(f32[64,384]{1,0:T(8,128)S(1)} %bitcast.12), channel_id=1, source_target_pairs={{8,7},{11,10},{14,13},{24,23},{27,26},{30,29},{40,39},{43,42},{46,... | collective-permute-start | bytes 294920 | tf_op jit(solution)/shard_map/ppermute | solution.py:347
  27.2 4.5 %collective-permute-start.5 = (f32[64,384]{1,0:T(8,128)S(1)}, f32[64,384]{1,0:T(8,128)S(1)}, u32[]{:S(2)}, u32[]{:S(2)}) collective-permute-start(f32[64,384]{1,0:T(8,128)S(1)} %get-tuple-element.50.refs_11_), channel_id=1, source_target_pairs={{5,7},{21,23},{37,39},{53,55},{69,71},{85,87},{101,103},{117,119},... | collective-permute-start | bytes 294920 | tf_op jit(solution)/shard_map/ppermute | solution.py:347
  31.7 0.7 copy-start.6
  31.7 2.7 %copy-start.13 = (f32[2,32,512]{2,1,0:T(8,128)S(1)}, f32[2,32,512]{2,1,0:T(8,128)}, u32[]{:S(2)}) copy-start(f32[2,32,512]{2,1,0:T(8,128)} %constant.15.clone.refs_1_) | copy-start | bytes 393220
  31.7 2.7 %copy-start.16 = (f32[2,16,512]{2,1,0:T(8,128)S(1)}, f32[2,16,512]{2,1,0:T(8,128)}, u32[]{:S(2)}) copy-start(f32[2,16,512]{2,1,0:T(8,128)} %constant.14.clone.refs_0_) | copy-start | bytes 196612
  31.7 2.7 %copy-start.17 = (f32[2,32,128]{2,1,0:T(8,128)S(1)}, f32[2,32,128]{2,1,0:T(8,128)}, u32[]{:S(2)}) copy-start(f32[2,32,128]{2,1,0:T(8,128)} %constant.17.clone.refs_3_) | copy-start | bytes 98308
  31.7 2.7 %copy-start.18 = (f32[2,16,128]{2,1,0:T(8,128)S(1)}, f32[2,16,128]{2,1,0:T(8,128)}, u32[]{:S(2)}) copy-start(f32[2,16,128]{2,1,0:T(8,128)} %constant.16.clone.refs_2_) | copy-start | bytes 49156
  31.7 4.6 %copy-start.10 = (bf16[2,128,128]{2,1,0:T(8,128)(2,1)S(1)}, bf16[2,128,128]{2,1,0:T(8,128)(2,1)}, u32[]{:S(2)}) copy-start(bf16[2,128,128]{2,1,0:T(8,128)(2,1)} %constant.18.clone.lanes_ref) | copy-start | bytes 196612
  32.4 0.7 copy-start.14
  33.1 9.5 %collective-permute-start.10 = (f32[64,384]{1,0:T(8,128)}, f32[64,384]{1,0:T(8,128)}, u32[]{:S(2)}, u32[]{:S(2)}) collective-permute-start(f32[64,384]{1,0:T(8,128)} %get-tuple-element.57.refs_11_), channel_id=1, source_target_pairs={{7,10},{23,26},{39,42},{55,58},{71,74},{87,90},{103,106},{119,122}... | collective-permute-start | bytes 294920 | tf_op jit(solution)/shard_map/ppermute | solution.py:347
  34.9 0.8 copy-start.2
  35.7 0.6 copy-start.8
  36.4 1.0 copy-start.3
  41.0 1.6 %copy-start.7 = (f32[64,384]{1,0:T(8,128)S(1)}, f32[64,384]{1,0:T(8,128)}, u32[]{:S(2)}) copy-start(f32[64,384]{1,0:T(8,128)} %copy-done.6) | copy-start | bytes 294916
  41.0 1.6 %copy-start.9 = (f32[64,384]{1,0:T(8,128)S(1)}, f32[64,384]{1,0:T(8,128)}, u32[]{:S(2)}) copy-start(f32[64,384]{1,0:T(8,128)} %copy-done.8) | copy-start | bytes 294916
  41.0 1.6 %copy-start.15 = (f32[64,384]{1,0:T(8,128)S(1)}, f32[64,384]{1,0:T(8,128)}, u32[]{:S(2)}) copy-start(f32[64,384]{1,0:T(8,128)} %copy-done.14) | copy-start | bytes 294916
  43.6 0.7 collective-permute-start.13
  44.3 2.2 %copy-start.1 = (f32[2,384,768]{2,1,0:T(8,128)S(1)}, f32[2,384,768]{2,1,0:T(8,128)}, u32[]{:S(2)}) copy-start(f32[2,384,768]{2,1,0:T(8,128)} %map_ref.3) | copy-start | bytes 7077892
  44.4 3.4 %collective-permute-start.14 = (f32[64,384]{1,0:T(8,128)S(1)}, f32[64,384]{1,0:T(8,128)S(1)}, u32[]{:S(2)}, u32[]{:S(2)}) collective-permute-start(f32[64,384]{1,0:T(8,128)S(1)} %get-tuple-element.70), channel_id=1, source_target_pairs={{5,6},{7,9},{10,12},{13,15},{21,22},{23,25},{26,28},{29,31},{37,38... | collective-permute-start | bytes 294920 | tf_op jit(solution)/shard_map/ppermute | solution.py:347
  45.2 1.7 %copy-start.19 = (s32[2,1024]{1,0:T(2,128)S(1)}, s32[2,1024]{1,0:T(2,128)}, u32[]{:S(2)}) copy-start(s32[2,1024]{1,0:T(2,128)} %pairs_ref.1) | copy-start | bytes 24580
  45.2 19.6 %collective-permute-start.15 = (f32[64,384]{1,0:T(8,128)S(1)}, f32[64,384]{1,0:T(8,128)S(1)}, u32[]{:S(2)}, u32[]{:S(2)}) collective-permute-start(f32[64,384]{1,0:T(8,128)S(1)} %get-tuple-element.71), channel_id=1, source_target_pairs={{7,8},{10,11},{13,14},{23,24},{26,27},{29,30},{39,40},{42,43},{45,... | collective-permute-start | bytes 294920 | tf_op jit(solution)/shard_map/ppermute | solution.py:347
  46.8 17.9 %copy-start.12 = (f32[2,768,32]{1,2,0:T(8,128)S(1)}, f32[2,768,32]{1,2,0:T(8,128)}, u32[]{:S(2)}) copy-start(f32[2,768,32]{1,2,0:T(8,128)} %param.14) | copy-start | bytes 589828
  64.8 29.9 %copy-start.4 = (f32[2,512,128]{2,1,0:T(8,128)S(1)}, f32[2,512,128]{2,1,0:T(8,128)}, u32[]{:S(2)}) copy-start(f32[2,512,128]{2,1,0:T(8,128)} %copy-done.2) | copy-start | bytes 1572868

commit v5 on v4

--- a/solution.py
+++ b/solution.py
@@ -16,16 +16,16 @@
 bf16 = jnp.bfloat16
 
 
-def call(kernel, out_shape, megabytes, scratch=(), awaits=False):
+def call(kernel, out_shape, megabytes, scratch=(), awaits=0):
     if awaits:
         vmem = pl.BlockSpec(memory_space=pltpu.VMEM)
 
         def after(*operands):
-            count = len(operands) - 1
-            specs = [vmem] * count + [pl.BlockSpec(memory_space=pl.ANY)]
+            count = len(operands) - awaits
+            specs = [vmem] * count + [pl.BlockSpec(memory_space=pl.ANY)] * awaits
 
             def body(*refs):
-                kernel(*refs[:count], *refs[count + 1 :])
+                kernel(*refs[:count], *refs[count + awaits :])
 
             return pl.pallas_call(
                 body,
@@ -74,7 +74,18 @@
 
 def split_map(value, *awaited):
     shape = jax.ShapeDtypeStruct((value.shape[1], 2 * value.shape[2]), bf16)
-    return call(split_kernel, [shape, shape], 8, (), bool(awaited))(value, *awaited)
+    return call(split_kernel, [shape, shape], 8, (), len(awaited))(value, *awaited)
+
+
+def split_both_kernel(first_ref, second_ref, *out_refs):
+    split_kernel(first_ref, *out_refs[:2])
+    split_kernel(second_ref, *out_refs[2:])
+
+
+def split_both(first, second, *awaited):
+    shape = jax.ShapeDtypeStruct((first.shape[1], 2 * first.shape[2]), bf16)
+    split = call(split_both_kernel, [shape] * 4, 10, (), len(awaited))
+    return split(first, second, *awaited)
 
 
 def advanced(state, high_ref, low_ref, source_ref):
@@ -184,7 +195,7 @@
 def pack_array(values, awaited):
     shape = jax.ShapeDtypeStruct((64, 8, 128), f32)
     scratch = [pltpu.VMEM((2, 8, 32, 128), f32)]
-    return call(pack_kernel, shape, 4, scratch, True)(values, awaited)
+    return call(pack_kernel, shape, 4, scratch, 1)(values, awaited)
 
 
 def unpack_array(packed):
@@ -202,9 +213,9 @@
             chosen_ref[:, column : column + 128] = jnp.where(rows == wanted, 1.0, 0.0).astype(bf16)
 
 
-def choose(pairs, orbitals):
+def choose(pairs, orbitals, *awaited):
     shape = jax.ShapeDtypeStruct((orbitals, 2 * pairs.shape[1]), bf16)
-    return call(choose_kernel, shape, 8)(pairs)
+    return call(choose_kernel, shape, 8, (), len(awaited))(pairs, *awaited)
 
 
 def lesser_kernel(
@@ -276,11 +287,11 @@
         twiddle_ref[1, rows] = jnp.where(lane < 64, turn, -turn)
 
 
-def tables(awaited):
+def tables(*awaited):
     *small, lanes = small_tables()
     waves = jax.ShapeDtypeStruct((512, 1024), bf16)
     shapes = [waves, waves, jax.ShapeDtypeStruct((2, 512, 128), f32)]
-    return (*call(tables_kernel, shapes, 8, (), True)(*small, awaited), lanes)
+    return (*call(tables_kernel, shapes, 8, (), len(awaited))(*small, *awaited), lanes)
 
 
 def turned(value):
@@ -368,20 +379,18 @@
     for order, leader in enumerate(LEADERS):
         arrived = move(state, (last, leader))
         if order < 2:
-            before, after = (split_map(value, *awaited) for value in maps[order])
-        operands = (arrived, *before, source_before, *own, *after, source_after)
+            split = split_both(*maps[order], *awaited)
+        operands = (arrived, *split[:2], source_before, *own, *split[2:], source_after)
         entering, middle, state = on_plane(
             triple_kernel, leader, place, operands, (entering, middle, state)
         )
-        if order == 0:
-            constants = tables(entering)
-            screened = screened_spectrum(screened, constants)
-            awaited = (screened,)
-        last = leader
+        last, awaited = leader, (entering,)
+    other = move(middle, *((leader, leader + 1) for leader in LEADERS))
     arrived = move(state, (SINGLES, SINGLES + 1), *((leader, leader + 2) for leader in LEADERS))
-    other = move(middle, *((leader, leader + 1) for leader in LEADERS))
-    local_high, local_low = split_map(local_map)
-    chosen = choose(element_pairs, local_map.shape[2])
+    constants = tables(screened, entering)
+    screened = screened_spectrum(screened, constants)
+    chosen = choose(element_pairs, local_map.shape[2], screened)
+    local_high, local_low = split_map(local_map, chosen)
     constant = jnp.swapaxes(local_source, 1, 2)
     packed = packed_lesser(arrived, other, entering, local_high, local_low, constant, chosen)
     result = convolve(exchange(packed), screened, constants)

time: 116 us -> 107 us (0.922)
  the two profiles are of different devices: /device:TPU:897 before, /device:TPU:833 now
where the time goes in v5:
time: 107 us; the launch traced here: 106 us
  blocking collectives  43.8 us (41%)
  starting transfers between devices  28.1 us (26%)
  waiting for transfers between devices  17.7 us (17%)
  Pallas kernels  13.8 us (13%)
  local copies, waits for them, and re-layouts  2.58 us (2%)
    all_to_all x2, blocking collectives, exchange(): lax.all_to_all(packed, 'energy', split_axis=0, concat_axis=0, tiled=True)  43.8 us
    ppermute x16, waiting for transfers between devices, move(): return lax.ppermute(value, 'space', pairs)  17.7 us
    ppermute x16, starting transfers between devices, move(): return lax.ppermute(value, 'space', pairs)  17.3 us
    all_to_all x1, starting transfers between devices, exchange(): lax.all_to_all(packed, 'energy', split_axis=0, concat_axis=0, tiled=True)  10.8 us
    pallas_call x5, Pallas kernels, after(): pl.pallas_call(body, out_shape=out_shape, in_specs=specs, scratch_shapes=...  4.62 us
    unnamed x22, local copies, waits for them, and re-layouts  2.58 us
  transfers between devices with their start and end apart: 17, of which 3 were waited for; matrix products, arithmetic and copies ran while one was open for 0% of the time, Pallas kernels for 9%

profile of v5, /device:TPU:833, one launch (start us, length us, event | category | flops | bytes accessed | tf_op | source)
XLA Modules:
  0.0 106.5 jit_solution(11980282937873198915)
XLA Ops:
  0.0 1.8 %collective-permute-start.7 = (f32[2,384,384]{2,1,0:T(8,128)}, f32[2,384,384]{2,1,0:T(8,128)}, u32[]{:S(2)}, u32[]{:S(2)}) collective-permute-start(f32[2,384,384]{2,1,0:T(8,128)} %map_ref.1), channel_id=1, source_target_pairs={{8,7},{24,23},{40,39},{56,55},{72,71},{88,87},{104,103},{120,119},... | collective-permute-start | bytes 3538952 | tf_op jit(solution)/shard_map/ppermute | solution.py:358
  1.8 1.7 %collective-permute-start.6 = (f32[2,384,384]{2,1,0:T(8,128)}, f32[2,384,384]{2,1,0:T(8,128)}, u32[]{:S(2)}, u32[]{:S(2)}) collective-permute-start(f32[2,384,384]{2,1,0:T(8,128)} %map_ref.1), channel_id=1, source_target_pairs={{6,7},{22,23},{38,39},{54,55},{70,71},{86,87},{102,103},{118,119},... | collective-permute-start | bytes 3538952 | tf_op jit(solution)/shard_map/ppermute | solution.py:358
  3.5 1.3 %collective-permute-start.12 = (f32[2,384,384]{2,1,0:T(8,128)}, f32[2,384,384]{2,1,0:T(8,128)S(1)}, u32[]{:S(2)}, u32[]{:S(2)}) collective-permute-start(f32[2,384,384]{2,1,0:T(8,128)} %map_ref.1), channel_id=1, source_target_pairs={{11,10},{14,13},{27,26},{30,29},{43,42},{46,45},{59,58},{62,61},{7... | collective-permute-start | bytes 3538952 | tf_op jit(solution)/shard_map/ppermute | solution.py:358
  4.8 1.3 %collective-permute-start.11 = (f32[2,384,384]{2,1,0:T(8,128)}, f32[2,384,384]{2,1,0:T(8,128)}, u32[]{:S(2)}, u32[]{:S(2)}) collective-permute-start(f32[2,384,384]{2,1,0:T(8,128)} %map_ref.1), channel_id=1, source_target_pairs={{9,10},{12,13},{25,26},{28,29},{41,42},{44,45},{57,58},{60,61},{73... | collective-permute-start | bytes 3538952 | tf_op jit(solution)/shard_map/ppermute | solution.py:358
  6.1 0.7 collective-permute-start
  6.8 0.0 copy-start.2
  6.8 1.3 %copy-done.2 = f32[2,384,384]{2,1,0:T(8,128)S(1)} copy-done((f32[2,384,384]{2,1,0:T(8,128)S(1)}, f32[2,384,384]{2,1,0:T(8,128)}, u32[]{:S(2)}) %copy-start.2) | copy-done | bytes 1179672
  8.0 0.2 shard_map.109
  8.3 0.0 collective-permute-done.arrived_ref
  8.3 0.0 copy-done
  8.3 0.7 collective-permute-start.1
  9.0 0.0 collective-permute-done.1.arrived_ref
  9.1 0.0 copy-start.4
  9.1 0.8 collective-permute-start.2
  9.9 0.0 collective-permute-done.2.arrived_ref
  9.9 0.7 collective-permute-start.3
  10.6 0.0 copy-done.4
  10.6 1.1 %shard_map.120 = f32[64,8,128]{2,1,0:T(8,128)} custom-call(f32[2,32,1024]{2,1,0:T(8,128)S(1)} %bitcast.16, f32[64,384]{1,0:T(8,128)S(1)} %get-tuple-element.47.refs_3_.refs_1_), custom_call_target="tpu_custom_call" | custom-call | tf_op jit(solution)/shard_map/pallas_call | solution.py:30
  11.7 10.8 %all-to-all-start = ((f32[64,8,128]{2,1,0:T(8,128)}), f32[64,8,128]{2,1,0:T(8,128)S(1)}, u32[]{:S(2)}, u32[]{:S(2)}) async-start(f32[64,8,128]{2,1,0:T(8,128)} %shard_map.120), calls=%async_computation | async-start | bytes 524288 | tf_op jit(solution)/shard_map/all_to_all | solution.py:349
  22.5 0.0 collective-permute-done.3.arrived_ref
  22.5 0.7 collective-permute-start.4
  23.2 0.0 collective-permute-done.4.arrived_ref
  23.2 1.3 %collective-permute-start.9 = (f32[64,384]{1,0:T(8,128)S(1)}, f32[64,384]{1,0:T(8,128)S(1)}, u32[]{:S(2)}, u32[]{:S(2)}) collective-permute-start(f32[64,384]{1,0:T(8,128)S(1)} %bitcast.10), channel_id=1, source_target_pairs={{8,7},{11,10},{14,13},{24,23},{27,26},{30,29},{40,39},{43,42},{46,... | collective-permute-start | bytes 294920 | tf_op jit(solution)/shard_map/ppermute | solution.py:358
  24.6 0.0 collective-permute-done.7.second_ref
  24.6 1.3 %collective-permute-start.8 = (f32[64,384]{1,0:T(8,128)S(1)}, f32[64,384]{1,0:T(8,128)S(1)}, u32[]{:S(2)}, u32[]{:S(2)}) collective-permute-start(f32[64,384]{1,0:T(8,128)S(1)} %bitcast.12), channel_id=1, source_target_pairs={{6,7},{9,10},{12,13},{22,23},{25,26},{28,29},{38,39},{41,42},{44,4... | collective-permute-start | bytes 294920 | tf_op jit(solution)/shard_map/ppermute | solution.py:358
  25.9 0.0 collective-permute-done.6.first_ref
  25.9 0.7 collective-permute-start.5
  26.5 2.1 %shard_map.115 = (bf16[384,768]{1,0:T(8,128)(2,1)S(1)}, bf16[384,768]{1,0:T(8,128)(2,1)S(1)}, bf16[384,768]{1,0:T(8,128)(2,1)S(1)}, bf16[384,768]{1,0:T(8,128)(2,1)S(1)}) custom-call(f32[2,384,384]{2,1,0:T(8,128)} %collective-permute-done.6.first_ref, f32[2,384,384]{2,1,0:T(8,128)} %collective-permute-done.7.second_ref), custom_call_target="tpu_custom_call" | custom-call | tf_op jit(solution)/shard_map/pallas_call | solution.py:88
  28.6 6.0 %collective-permute-done.9.refs_8_ = f32[64,384]{1,0:T(8,128)S(1)} collective-permute-done((f32[64,384]{1,0:T(8,128)S(1)}, f32[64,384]{1,0:T(8,128)S(1)}, u32[]{:S(2)}, u32[]{:S(2)}) %collective-permute-start.9) | collective-permute-done | bytes 98336 | tf_op jit(solution)/shard_map/ppermute | solution.py:358
  34.7 1.3 %collective-permute-done.8.refs_2_ = f32[64,384]{1,0:T(8,128)S(1)} collective-permute-done((f32[64,384]{1,0:T(8,128)S(1)}, f32[64,384]{1,0:T(8,128)S(1)}, u32[]{:S(2)}, u32[]{:S(2)}) %collective-permute-start.8) | collective-permute-done | bytes 98336 | tf_op jit(solution)/shard_map/ppermute | solution.py:358
  36.0 0.0 collective-permute-done.5.arrived_ref
  36.0 0.7 collective-permute-start.10
  36.7 0.0 collective-permute-done.12.refs_1_
  36.7 0.0 collective-permute-done.11.refs_0_
  36.7 1.7 %shard_map.117 = (bf16[384,768]{1,0:T(8,128)(2,1)S(1)}, bf16[384,768]{1,0:T(8,128)(2,1)S(1)}, bf16[384,768]{1,0:T(8,128)(2,1)S(1)}, bf16[384,768]{1,0:T(8,128)(2,1)S(1)}) custom-call(f32[2,384,384]{2,1,0:T(8,128)} %collective-permute-done.11.refs_0_, f32[2,384,384]{2,1,0:T(8,128)S(1)} %collective-permute-done.12.refs_1_, ...), custom_call_target="tpu_custom_call" | custom-call | tf_op jit(solution)/shard_map/pallas_call | solution.py:30
  38.4 0.0 collective-permute-done.10.arrived_ref
  38.5 1.3 %collective-permute-start.13 = (f32[64,384]{1,0:T(8,128)S(1)}, f32[64,384]{1,0:T(8,128)S(1)}, u32[]{:S(2)}, u32[]{:S(2)}) collective-permute-start(f32[64,384]{1,0:T(8,128)S(1)} %get-tuple-element.64.refs_11_), channel_id=1, source_target_pairs={{10,13},{26,29},{42,45},{58,61},{74,77},{90,93},{106,109},{122,125... | collective-permute-start | bytes 294920 | tf_op jit(solution)/shard_map/ppermute | solution.py:358
  39.8 10.4 %collective-permute-done.13.arrived_ref = f32[64,384]{1,0:T(8,128)S(1)} collective-permute-done((f32[64,384]{1,0:T(8,128)S(1)}, f32[64,384]{1,0:T(8,128)S(1)}, u32[]{:S(2)}, u32[]{:S(2)}) %collective-permute-start.13) | collective-permute-done | bytes 98336 | tf_op jit(solution)/shard_map/ppermute | solution.py:358
  50.2 0.0 copy-start.3
  50.2 1.0 shard_map.119
  51.2 1.3 %collective-permute-start.14 = (f32[64,384]{1,0:T(8,128)S(1)}, f32[64,384]{1,0:T(8,128)S(1)}, u32[]{:S(2)}, u32[]{:S(2)}) collective-permute-start(f32[64,384]{1,0:T(8,128)S(1)} %get-tuple-element.67), channel_id=1, source_target_pairs={{5,6},{7,9},{10,12},{13,15},{21,22},{23,25},{26,28},{29,31},{37,38... | collective-permute-start | bytes 294920 | tf_op jit(solution)/shard_map/ppermute | solution.py:358
  52.5 1.3 %collective-permute-start.15 = (f32[64,384]{1,0:T(8,128)S(1)}, f32[64,384]{1,0:T(8,128)S(1)}, u32[]{:S(2)}, u32[]{:S(2)}) collective-permute-start(f32[64,384]{1,0:T(8,128)S(1)} %get-tuple-element.68), channel_id=1, source_target_pairs={{7,8},{10,11},{13,14},{23,24},{26,27},{29,30},{39,40},{42,43},{45,... | collective-permute-start | bytes 294920 | tf_op jit(solution)/shard_map/ppermute | solution.py:358
  53.8 0.0 all-to-all-done.refs_4_.packed_ref
  53.8 0.0 copy-done.6
  53.8 0.0 copy-done.7
  53.9 0.0 copy-done.8
  53.9 0.0 copy-done.9
  53.9 0.5 shard_map.121
  54.4 0.0 copy-done.3
  54.4 0.0 copy-start.10
  54.4 1.1 %shard_map.122.refs_1_.screened_ref = f32[2,512,128]{2,1,0:T(8,128)S(1)} custom-call(f32[64,8,128]{2,1,0:T(8,128)S(1)} %all-to-all-done.refs_4_.packed_ref, bf16[512,1024]{1,0:T(8,128)(2,1)S(1)} %get-tuple-element.70.high_ref, bf16[512,1024]{1,0:T(8,128)(2,1)S(1)} %get-tuple-element.71.low_ref, f32[2,512,128]{2,1,0:T(8,128)S(1)} %get-tuple-element.72.twiddle_ref, ...), custom_call_target="tpu_custom_call" | custom-call | tf_op jit(solution)/shard_map/pallas_call | solution.py:340
  55.6 0.0 copy-done.10
  55.6 0.0 copy-start.1
  55.6 1.0 shard_map.123.refs_1_.chosen_ref
  56.6 0.7 copy-done.1
  57.3 0.3 shard_map.124
  57.6 0.0 collective-permute-done.14.arrived_ref
  57.6 0.0 collective-permute-done.15.other_ref
  57.6 0.6 copy-done.5
  58.2 1.4 %shard_map.125 = f32[64,8,128]{2,1,0:T(8,128)S(1)} custom-call(f32[64,384]{1,0:T(8,128)S(1)} %collective-permute-done.14.arrived_ref, f32[64,384]{1,0:T(8,128)S(1)} %collective-permute-done.15.other_ref, f32[64,384]{1,0:T(8,128)S(1)} %get-tuple-element.69.refs_5_.entering_ref, bf16[384,1536]{1,0:T(8,128)(2,1)S(1)} %get-tuple-element.73.high_ref, ...), custom_call_target="tpu_custom_call" | custom-call | tf_op jit(solution)/shard_map/pallas_call | solution.py:245
  59.6 26.0 %all_to_all.15.packed_ref = f32[64,8,128]{2,1,0:T(8,128)S(1)} all-to-all(f32[64,8,128]{2,1,0:T(8,128)S(1)} %shard_map.125), channel_id=1, replica_groups=mesh['energy'=64,'space'=16] {'energy'}, dimensions={0} | all-to-all | bytes 524288 | tf_op jit(solution)/shard_map/all_to_all | solution.py:349
  85.6 2.0 %shard_map.126 = f32[64,8,128]{2,1,0:T(8,128)S(1)} custom-call(f32[64,8,128]{2,1,0:T(8,128)S(1)} %all_to_all.15.packed_ref, f32[2,512,128]{2,1,0:T(8,128)S(1)} %shard_map.122.refs_1_.screened_ref, bf16[512,1024]{1,0:T(8,128)(2,1)S(1)} %get-tuple-element.70.high_ref, bf16[512,1024]{1,0:T(8,128)(2,1)S(1)} %get-tuple-element.71.low_ref, ...), custom_call_target="tpu_custom_call" | custom-call | tf_op jit(solution)/shard_map/pallas_call | solution.py:345
  87.6 17.8 %all_to_all.16.packed_ref = f32[64,8,128]{2,1,0:T(8,128)S(1)} all-to-all(f32[64,8,128]{2,1,0:T(8,128)S(1)} %shard_map.126), channel_id=1, replica_groups=mesh['energy'=64,'space'=16] {'energy'}, dimensions={0} | all-to-all | bytes 524288 | tf_op jit(solution)/shard_map/all_to_all | solution.py:349
  105.4 1.1 %shard_map.127 = f32[2,32,1024]{2,1,0:T(8,128)} custom-call(f32[64,8,128]{2,1,0:T(8,128)S(1)} %all_to_all.16.packed_ref), custom_call_target="tpu_custom_call" | custom-call | tf_op jit(solution)/shard_map/pallas_call | solution.py:203
  (13 shorter events, 0.2 us)
Async XLA Ops:
  0.0 8.3 %copy-start = (f32[2,32,384]{2,1,0:T(8,128)S(1)}, f32[2,32,384]{2,1,0:T(8,128)}, u32[]{:S(2)}) copy-start(f32[2,32,384]{2,1,0:T(8,128)} %param.12) | copy-start | bytes 294916
  0.0 24.6 %collective-permute-start.7 = (f32[2,384,384]{2,1,0:T(8,128)}, f32[2,384,384]{2,1,0:T(8,128)}, u32[]{:S(2)}, u32[]{:S(2)}) collective-permute-start(f32[2,384,384]{2,1,0:T(8,128)} %map_ref.1), channel_id=1, source_target_pairs={{8,7},{24,23},{40,39},{56,55},{72,71},{88,87},{104,103},{120,119},... | collective-permute-start | bytes 3538952 | tf_op jit(solution)/shard_map/ppermute | solution.py:358
  1.8 24.1 %collective-permute-start.6 = (f32[2,384,384]{2,1,0:T(8,128)}, f32[2,384,384]{2,1,0:T(8,128)}, u32[]{:S(2)}, u32[]{:S(2)}) collective-permute-start(f32[2,384,384]{2,1,0:T(8,128)} %map_ref.1), channel_id=1, source_target_pairs={{6,7},{22,23},{38,39},{54,55},{70,71},{86,87},{102,103},{118,119},... | collective-permute-start | bytes 3538952 | tf_op jit(solution)/shard_map/ppermute | solution.py:358
  3.5 33.2 %collective-permute-start.12 = (f32[2,384,384]{2,1,0:T(8,128)}, f32[2,384,384]{2,1,0:T(8,128)S(1)}, u32[]{:S(2)}, u32[]{:S(2)}) collective-permute-start(f32[2,384,384]{2,1,0:T(8,128)} %map_ref.1), channel_id=1, source_target_pairs={{11,10},{14,13},{27,26},{30,29},{43,42},{46,45},{59,58},{62,61},{7... | collective-permute-start | bytes 3538952 | tf_op jit(solution)/shard_map/ppermute | solution.py:358
  4.8 31.9 %collective-permute-start.11 = (f32[2,384,384]{2,1,0:T(8,128)}, f32[2,384,384]{2,1,0:T(8,128)}, u32[]{:S(2)}, u32[]{:S(2)}) collective-permute-start(f32[2,384,384]{2,1,0:T(8,128)} %map_ref.1), channel_id=1, source_target_pairs={{9,10},{12,13},{25,26},{28,29},{41,42},{44,45},{57,58},{60,61},{73... | collective-permute-start | bytes 3538952 | tf_op jit(solution)/shard_map/ppermute | solution.py:358
  6.1 2.2 %collective-permute-start = (f32[64,384]{1,0:T(8,128)}, f32[64,384]{1,0:T(8,128)S(1)}, u32[]{:S(2)}, u32[]{:S(2)}) collective-permute-start(f32[64,384]{1,0:T(8,128)} %bitcast.5), channel_id=1, source_target_pairs={{0,1},{16,17},{32,33},{48,49},{64,65},{80,81},{96,97},{112,113},{1... | collective-permute-start | bytes 294920 | tf_op jit(solution)/shard_map/ppermute | solution.py:358
  6.8 1.3 %copy-start.2 = (f32[2,384,384]{2,1,0:T(8,128)S(1)}, f32[2,384,384]{2,1,0:T(8,128)}, u32[]{:S(2)}) copy-start(f32[2,384,384]{2,1,0:T(8,128)} %map_ref.1) | copy-start | bytes 3538948
  8.3 0.7 collective-permute-start.1
  9.1 1.5 %copy-start.4 = (f32[2,1024,32]{1,2,0:T(8,128)S(1)}, f32[2,1024,32]{1,2,0:T(8,128)}, u32[]{:S(2)}) copy-start(f32[2,1024,32]{1,2,0:T(8,128)} %param.15) | copy-start | bytes 786436
  9.1 0.8 collective-permute-start.2
  9.9 12.6 %collective-permute-start.3 = (f32[64,384]{1,0:T(8,128)S(1)}, f32[64,384]{1,0:T(8,128)S(1)}, u32[]{:S(2)}, u32[]{:S(2)}) collective-permute-start(f32[64,384]{1,0:T(8,128)S(1)} %get-tuple-element.46.refs_4_), channel_id=1, source_target_pairs={{3,4},{19,20},{35,36},{51,52},{67,68},{83,84},{99,100},{115,116},{... | collective-permute-start | bytes 294920 | tf_op jit(solution)/shard_map/ppermute | solution.py:358
  11.7 42.1 %all-to-all-start = ((f32[64,8,128]{2,1,0:T(8,128)}), f32[64,8,128]{2,1,0:T(8,128)S(1)}, u32[]{:S(2)}, u32[]{:S(2)}) async-start(f32[64,8,128]{2,1,0:T(8,128)} %shard_map.120), calls=%async_computation | async-start | bytes 524288 | tf_op jit(solution)/shard_map/all_to_all | solution.py:349
  22.5 0.7 collective-permute-start.4
  23.2 11.4 %collective-permute-start.9 = (f32[64,384]{1,0:T(8,128)S(1)}, f32[64,384]{1,0:T(8,128)S(1)}, u32[]{:S(2)}, u32[]{:S(2)}) collective-permute-start(f32[64,384]{1,0:T(8,128)S(1)} %bitcast.10), channel_id=1, source_target_pairs={{8,7},{11,10},{14,13},{24,23},{27,26},{30,29},{40,39},{43,42},{46,... | collective-permute-start | bytes 294920 | tf_op jit(solution)/shard_map/ppermute | solution.py:358
  24.6 11.4 %collective-permute-start.8 = (f32[64,384]{1,0:T(8,128)S(1)}, f32[64,384]{1,0:T(8,128)S(1)}, u32[]{:S(2)}, u32[]{:S(2)}) collective-permute-start(f32[64,384]{1,0:T(8,128)S(1)} %bitcast.12), channel_id=1, source_target_pairs={{6,7},{9,10},{12,13},{22,23},{25,26},{28,29},{38,39},{41,42},{44,4... | collective-permute-start | bytes 294920 | tf_op jit(solution)/shard_map/ppermute | solution.py:358
  25.9 10.1 %collective-permute-start.5 = (f32[64,384]{1,0:T(8,128)S(1)}, f32[64,384]{1,0:T(8,128)S(1)}, u32[]{:S(2)}, u32[]{:S(2)}) collective-permute-start(f32[64,384]{1,0:T(8,128)S(1)} %get-tuple-element.50.refs_11_), channel_id=1, source_target_pairs={{5,7},{21,23},{37,39},{53,55},{69,71},{85,87},{101,103},{117,119},... | collective-permute-start | bytes 294920 | tf_op jit(solution)/shard_map/ppermute | solution.py:358
  36.0 2.4 %collective-permute-start.10 = (f32[64,384]{1,0:T(8,128)S(1)}, f32[64,384]{1,0:T(8,128)S(1)}, u32[]{:S(2)}, u32[]{:S(2)}) collective-permute-start(f32[64,384]{1,0:T(8,128)S(1)} %get-tuple-element.57.refs_11_), channel_id=1, source_target_pairs={{7,10},{23,26},{39,42},{55,58},{71,74},{87,90},{103,106},{119,122}... | collective-permute-start | bytes 294920 | tf_op jit(solution)/shard_map/ppermute | solution.py:358
  38.5 11.7 %collective-permute-start.13 = (f32[64,384]{1,0:T(8,128)S(1)}, f32[64,384]{1,0:T(8,128)S(1)}, u32[]{:S(2)}, u32[]{:S(2)}) collective-permute-start(f32[64,384]{1,0:T(8,128)S(1)} %get-tuple-element.64.refs_11_), channel_id=1, source_target_pairs={{10,13},{26,29},{42,45},{58,61},{74,77},{90,93},{106,109},{122,125... | collective-permute-start | bytes 294920 | tf_op jit(solution)/shard_map/ppermute | solution.py:358
  50.1 3.7 %copy-start.6 = (f32[2,32,512]{2,1,0:T(8,128)S(1)}, f32[2,32,512]{2,1,0:T(8,128)}, u32[]{:S(2)}) copy-start(f32[2,32,512]{2,1,0:T(8,128)} %constant.15.clone.refs_1_) | copy-start | bytes 393220
  50.1 3.7 %copy-start.7 = (f32[2,16,512]{2,1,0:T(8,128)S(1)}, f32[2,16,512]{2,1,0:T(8,128)}, u32[]{:S(2)}) copy-start(f32[2,16,512]{2,1,0:T(8,128)} %constant.14.clone.refs_0_) | copy-start | bytes 196612
  50.2 3.7 %copy-start.8 = (f32[2,32,128]{2,1,0:T(8,128)S(1)}, f32[2,32,128]{2,1,0:T(8,128)}, u32[]{:S(2)}) copy-start(f32[2,32,128]{2,1,0:T(8,128)} %constant.17.clone.refs_3_) | copy-start | bytes 98308
  50.2 3.7 %copy-start.9 = (f32[2,16,128]{2,1,0:T(8,128)S(1)}, f32[2,16,128]{2,1,0:T(8,128)}, u32[]{:S(2)}) copy-start(f32[2,16,128]{2,1,0:T(8,128)} %constant.16.clone.refs_2_) | copy-start | bytes 49156
  50.2 4.3 %copy-start.3 = (bf16[2,128,128]{2,1,0:T(8,128)(2,1)S(1)}, bf16[2,128,128]{2,1,0:T(8,128)(2,1)}, u32[]{:S(2)}) copy-start(bf16[2,128,128]{2,1,0:T(8,128)(2,1)} %constant.18.clone.lanes_ref) | copy-start | bytes 196612
  51.2 6.4 %collective-permute-start.14 = (f32[64,384]{1,0:T(8,128)S(1)}, f32[64,384]{1,0:T(8,128)S(1)}, u32[]{:S(2)}, u32[]{:S(2)}) collective-permute-start(f32[64,384]{1,0:T(8,128)S(1)} %get-tuple-element.67), channel_id=1, source_target_pairs={{5,6},{7,9},{10,12},{13,15},{21,22},{23,25},{26,28},{29,31},{37,38... | collective-permute-start | bytes 294920 | tf_op jit(solution)/shard_map/ppermute | solution.py:358
  52.5 5.1 %collective-permute-start.15 = (f32[64,384]{1,0:T(8,128)S(1)}, f32[64,384]{1,0:T(8,128)S(1)}, u32[]{:S(2)}, u32[]{:S(2)}) collective-permute-start(f32[64,384]{1,0:T(8,128)S(1)} %get-tuple-element.68), channel_id=1, source_target_pairs={{7,8},{10,11},{13,14},{23,24},{26,27},{29,30},{39,40},{42,43},{45,... | collective-permute-start | bytes 294920 | tf_op jit(solution)/shard_map/ppermute | solution.py:358
  54.4 1.1 %copy-start.10 = (s32[2,1024]{1,0:T(2,128)S(1)}, s32[2,1024]{1,0:T(2,128)}, u32[]{:S(2)}) copy-start(s32[2,1024]{1,0:T(2,128)} %refs_0_.3) | copy-start | bytes 24580
  55.6 1.7 %copy-start.1 = (f32[2,384,768]{2,1,0:T(8,128)S(1)}, f32[2,384,768]{2,1,0:T(8,128)}, u32[]{:S(2)}) copy-start(f32[2,384,768]{2,1,0:T(8,128)} %refs_0_.4) | copy-start | bytes 7077892
  57.3 0.9 copy-start.5
